TPU v7x, 32 devices: a whole 2x2x4 slice. The times are simulated.
32 devices in a mesh: cube: 4 (over z), front: 8 (over y, x, core).
Axes of the slice: x: 2, y: 2, z: 4, core: 2. Of those that a mesh axis runs over, the one named last changes fastest.
Arguments:
- right_sides: float32 [3, 4, 512, 128], P(None, 'cube', 'front'), may hold values from -6 to 6
- inverse_leaf: float32 [4, 512, 512], P('cube', 'front'), may hold values from -2 to 2, as said below
- inverse_mid: float32 [4, 512, 1024], P('cube', 'front'), may hold values from -2 to 2, as said below
- inverse_top: float32 [4, 512, 2048], P('cube', 'front'), may hold values from -2 to 2, as said below
- coupling_mid: float32 [4, 512, 1024], P('cube', 'front'), may hold values from -0.25 to 0.25
- coupling_top: float32 [4, 512, 2048], P('cube', 'front'), may hold values from -0.1875 to 0.1875
- pattern_mid: int32 [4, 8, 16], P('cube', 'front'), may hold values 0 or 1
- pattern_top: int32 [4, 8, 32], P('cube', 'front'), may hold values 0 or 1
Outputs:
- solution: float32 [3, 4, 512, 128], P(None, 'cube', 'front')
Inputs may be any that keep to these rules, and one draw needn't show every extreme that they name: `inverse_leaf`: each block is the inverse of a lower triangular diagonal block: zero above the diagonal of the separator's row order, diagonal 1 to 2. `inverse_mid`: as inverse_leaf. `inverse_top`: as inverse_leaf.
All inputs are finite; a program needn't handle non-finite values. No bound on the sum of `pattern_mid` or of `pattern_top` on one device may be relied on, other than what follows from the above.
Results may differ from a plain program's by a relative error of at most 0.00013.
Values sent between devices are 32-bit elements; how exact they have to be, the bound alone decides.
No kernel may reach another device: no remote copies, remote signals or barrier semaphores. Data moves between devices by JAX's collectives and lax.ppermute only.
A program may use at most 64 MiB of HBM per device.

v0:
```python
import jax
import jax.numpy as jnp
from jax import lax
from jax.sharding import PartitionSpec as P

TILE = 64
TEAM = 4


def exchange(value, axis, mask):
    pairs = [(source, source ^ mask) for source in range(lax.axis_size(axis))]
    return lax.ppermute(value, axis, pairs)


def absolute(pieces, index, axis=0):
    count, bit = len(pieces), 1
    while bit < count:
        pieces = [
            jnp.where(index // bit % 2 == 0, pieces[m], pieces[m ^ bit]) for m in range(count)
        ]
        bit *= 2
    return jnp.stack(pieces, axis)


def team_order(pieces, g):
    join = lambda a, b: jnp.concatenate([a, b], axis=-1)
    inner = [
        jnp.where(g % 2 == 0, join(pieces[m], pieces[m + 1]), join(pieces[m + 1], pieces[m]))
        for m in (0, 2)
    ]
    return jnp.where(g // 2 == 0, join(*inner), join(inner[1], inner[0]))


def team_pieces(value, g):
    half = value.shape[-1] // 2
    sides = value[..., :half], value[..., half:]
    pieces = []
    for first, second in (sides, sides[::-1]):
        same = jnp.where(g // 2 == 0, first, second)
        parts = same[..., : half // 2], same[..., half // 2 :]
        for a, b in (parts, parts[::-1]):
            pieces.append(jnp.where(g % 2 == 0, a, b))
    return pieces


def to_parts(pieces, axis, unit):
    return [piece if m == 0 else exchange(piece, axis, m * unit) for m, piece in enumerate(pieces)]


def summed(value, axis, count, unit):
    bit = 1
    while bit < count:
        value = value + exchange(value, axis, bit * unit)
        bit *= 2
    return value


def times(vector, matrix, contract):
    return lax.dot_general(
        vector, matrix, (((1,), (contract,)), ((), ())), precision=lax.Precision.HIGHEST,
        preferred_element_type=jnp.float32,
    )


def local(
    right_sides,
    inverse_leaf,
    inverse_mid,
    inverse_top,
    coupling_mid,
    coupling_top,
    pattern_mid,
    pattern_top,
):
    front = lax.axis_size("front")
    cube_pos, front_pos = lax.axis_index("cube"), lax.axis_index("front")
    parts = front // TEAM
    g, q = front_pos % TEAM, front_pos // TEAM
    _, _, rows, columns = right_sides.shape
    width, half, full = columns // TEAM, TEAM * rows, front * rows
    group_mid, group_top = inverse_mid.shape[2] // full, inverse_top.shape[2] // full

    def inverse_pieces(inverse, count):
        return [
            jnp.concatenate([
                lax.dynamic_slice_in_dim(inverse[0], (block * parts + (q ^ m)) * half, half, 1)
                for block in range(count)
            ], axis=1)
            for m in range(parts)
        ]

    def coupling_pieces(coupling, pattern, count):
        keep = jnp.repeat(pattern[0].astype(jnp.float32), TILE, axis=1)
        starts = [(cube_pos % count ^ m) * full for m in range(count)]
        return [
            lax.dynamic_slice_in_dim(coupling[0], start, full, 1)
            * lax.dynamic_slice_in_dim(keep, start, full, 1)
            for start in starts
        ]

    def whole_block(own, across):
        if across is None:
            across = exchange(own, "front", 2)
        beside = exchange(own, "front", 1)
        both = exchange(across, "front", 1)
        whole = absolute([own, beside, across, both], g, axis=1)
        return whole.reshape(TEAM * own.shape[0] * rows, own.shape[2])

    def inverse_block(inverse, count):
        pieces = inverse_pieces(inverse, count)
        own = absolute(to_parts(pieces, "front", TEAM), q)
        return whole_block(own, None)

    def coupling_block(coupling, pattern, count):
        pieces = coupling_pieces(coupling, pattern, count)
        own = absolute(to_parts(pieces, "cube", 1), cube_pos % count)
        return whole_block(own, None)

    def own_rows(side, count):
        here = lax.broadcasted_iota(jnp.int32, (1, count, 1), 1) == cube_pos % count
        return jnp.where(here, side[:, None], 0.0).reshape(width, count * half)

    def pick(value, count):
        return lax.dynamic_slice_in_dim(value, cube_pos % count * half, half, 1)

    def rows_back(value):
        pieces = to_parts(team_pieces(value, g), "front", 1)
        turned = absolute(pieces, g, axis=1).reshape(value.shape[0], columns, rows)
        return jnp.swapaxes(turned, 1, 2)

    pieces = inverse_pieces(inverse_leaf, 1)
    own = absolute(to_parts(pieces, "front", TEAM), q)
    across = absolute([exchange(piece, "front", m * TEAM + 2) for m, piece in enumerate(pieces)], q)
    turned = jnp.swapaxes(right_sides[:, 0], 1, 2)
    sides = team_order(to_parts([
        lax.dynamic_slice_in_dim(turned, (g ^ m) * width, width, 1) for m in range(TEAM)
    ], "front", 1), g)

    leaf = whole_block(own, across)
    couple_mid = coupling_block(coupling_mid, pattern_mid, group_mid)
    mid = inverse_block(inverse_mid, group_mid)
    couple_top = coupling_block(coupling_top, pattern_top, group_top)
    top = inverse_block(inverse_top, group_top)

    y0 = summed(times(sides[0], leaf, 1), "front", parts, TEAM)
    w1 = own_rows(sides[1], group_mid) - times(y0, couple_mid, 1)
    w1 = summed(w1, "cube", group_mid, 1)
    y1 = summed(times(w1, mid, 1), "front", parts, TEAM)
    w2 = own_rows(sides[2], group_top) - times(y1, couple_top, 1)
    w2 = summed(w2, "cube", group_top, 1)
    y2 = summed(times(w2, top, 1), "front", parts, TEAM)
    x2 = summed(times(y2, top, 0), "cube", group_top, 1)
    c1 = summed(times(x2, couple_top, 0), "front", parts, TEAM)
    x1 = summed(times(y1 - c1, mid, 0), "cube", group_mid, 1)
    c0 = summed(times(x1, couple_mid, 0), "front", parts, TEAM)
    upper = rows_back(jnp.stack([pick(x1, group_mid), pick(x2, group_top)]))
    x0 = times(y0 - c0, leaf, 0)
    return jnp.concatenate([rows_back(x0[None]), upper])[:, None]


def solution(mesh):
    return jax.shard_map(
        local,
        mesh=mesh,
        in_specs=(
            P(None, "cube", "front", None),
            P("cube", "front", None),
            P("cube", "front", None),
            P("cube", "front", None),
            P("cube", "front", None),
            P("cube", "front", None),
            P("cube", "front", None),
            P("cube", "front", None),
        ),
        out_specs=P(None, "cube", "front", None),
        check_vma=False,
    )
```

profile of v0, /device:TPU:0, one launch (start us, length us, event | category | flops | bytes accessed | tf_op | source)
XLA Modules:
  0.0 135.3 jit_solution(8044748867012285680)
XLA Ops:
  0.1 1.6 %dynamic-slice_bitcast_fusion.12 = f32[64,256]{1,0:T(8,128)} fusion(f32[1,64,512]{2,1,0:T(8,128)} %param.9, s32[]{:T(128)S(6)} %select_n.844), kind=kLoop, calls=%fused_computation.105 | loop fusion | bytes 131076 | tf_op jit(solution)/shard_map/dynamic_slice | solution.py:86
  1.6 3.0 %collective-permute-start.3 = (f32[64,256]{1,0:T(8,128)}, f32[64,256]{1,0:T(8,128)S(1)}, u32[]{:S(2)}, u32[]{:S(2)}) collective-permute-start(f32[64,256]{1,0:T(8,128)} %dynamic-slice_bitcast_fusion.12), channel_id=1, source_target_pairs={{0,4},{1,5},{2,6},{3,7},{4,0},{5,1},{6,2},{7,3},{8,12},{9,13},{10,... | collective-permute-start | bytes 196616 | tf_op jit(solution)/shard_map/ppermute | solution.py:12
  4.6 1.4 %collective-permute-start.6 = (f32[64,256]{1,0:T(8,128)}, f32[64,256]{1,0:T(8,128)}, u32[]{:S(2)}, u32[]{:S(2)}) collective-permute-start(f32[64,256]{1,0:T(8,128)} %dynamic-slice_bitcast_fusion.12), channel_id=1, source_target_pairs={{0,6},{1,7},{2,4},{3,5},{4,2},{5,3},{6,0},{7,1},{8,14},{9,15},{10,... | collective-permute-start | bytes 196616 | tf_op jit(solution)/shard_map/ppermute | solution.py:12
  6.1 1.1 dynamic-slice_bitcast_fusion.7
  7.2 1.6 %collective-permute-start.27 = (f32[64,1024]{1,0:T(8,128)S(1)}, f32[64,1024]{1,0:T(8,128)S(1)}, u32[]{:S(2)}, u32[]{:S(2)}) collective-permute-start(f32[64,1024]{1,0:T(8,128)S(1)} %pad_maximum_fusion.10), channel_id=1, source_target_pairs={{0,4},{1,5},{2,6},{3,7},{4,0},{5,1},{6,2},{7,3},{8,12},{9,13},{10,... | collective-permute-start | bytes 786440 | tf_op jit(solution)/shard_map/ppermute | solution.py:12
  11.1 1.5 %collective-permute-done.2 = f32[3,32,64]{2,1,0:T(8,128)S(1)} collective-permute-done((f32[3,32,64]{2,1,0:T(8,128)S(1)}, f32[3,32,64]{2,1,0:T(8,128)S(1)}, u32[]{:S(2)}, u32[]{:S(2)}) %collective-permute-start.2) | collective-permute-done | bytes 24608 | tf_op jit(solution)/shard_map/ppermute | solution.py:12
  13.8 1.1 collective-permute-done
  14.9 1.6 %collective-permute-start.9 = (f32[64,512]{1,0:T(8,128)S(1)}, f32[64,512]{1,0:T(8,128)S(1)}, u32[]{:S(2)}, u32[]{:S(2)}) collective-permute-start(f32[64,512]{1,0:T(8,128)S(1)} %bitcast_multiply_fusion.4), channel_id=1, source_target_pairs={{0,8},{8,0},{16,24},{24,16},{1,9},{9,1},{17,25},{25,17},{2,10},{10... | collective-permute-start | bytes 393224 | tf_op jit(solution)/shard_map/ppermute | solution.py:12
  17.3 2.7 %collective-permute-start.20 = (f32[64,512]{1,0:T(8,128)S(1)}, f32[64,512]{1,0:T(8,128)S(1)}, u32[]{:S(2)}, u32[]{:S(2)}) collective-permute-start(f32[64,512]{1,0:T(8,128)S(1)} %get-tuple-element.32), channel_id=1, source_target_pairs={{0,16},{8,24},{16,0},{24,8},{1,17},{9,25},{17,1},{25,9},{2,18},{10... | collective-permute-start | bytes 393224 | tf_op jit(solution)/shard_map/ppermute | solution.py:12
  20.9 2.0 %collective-permute-start.21 = (f32[64,512]{1,0:T(8,128)S(1)}, f32[64,512]{1,0:T(8,128)S(1)}, u32[]{:S(2)}, u32[]{:S(2)}) collective-permute-start(f32[64,512]{1,0:T(8,128)S(1)} %get-tuple-element.31), channel_id=1, source_target_pairs={{0,24},{8,16},{16,8},{24,0},{1,25},{9,17},{17,9},{25,1},{2,26},{10... | collective-permute-start | bytes 393224 | tf_op jit(solution)/shard_map/ppermute | solution.py:12
  22.9 1.4 %collective-permute-done.5 = f32[64,256]{1,0:T(8,128)S(1)} collective-permute-done((f32[64,256]{1,0:T(8,128)S(1)}, f32[64,256]{1,0:T(8,128)S(1)}, u32[]{:S(2)}, u32[]{:S(2)}) %collective-permute-start.5) | collective-permute-done | bytes 65568 | tf_op jit(solution)/shard_map/ppermute | solution.py:12
  25.8 4.4 %collective-permute-done.20 = f32[64,512]{1,0:T(8,128)S(1)} collective-permute-done((f32[64,512]{1,0:T(8,128)S(1)}, f32[64,512]{1,0:T(8,128)S(1)}, u32[]{:S(2)}, u32[]{:S(2)}) %collective-permute-start.20) | collective-permute-done | bytes 131104 | tf_op jit(solution)/shard_map/ppermute | solution.py:12
  33.4 1.0 collective-permute-start.11
  35.1 1.1 collective-permute-start.8
  36.2 8.4 %collective-permute-done.11 = f32[2,64,512]{2,1,0:T(8,128)S(1)} collective-permute-done((f32[2,64,512]{2,1,0:T(8,128)S(1)}, f32[2,64,512]{2,1,0:T(8,128)S(1)}, u32[]{:S(2)}, u32[]{:S(2)}) %collective-permute-start.11) | collective-permute-done | bytes 262176 | tf_op jit(solution)/shard_map/ppermute | solution.py:12
  46.0 1.0 collective-permute-start.23
  47.0 1.1 collective-permute-start.29
  48.4 1.0 convolution_subtract_fusion.1
  49.5 1.0 collective-permute-start.13
  50.5 10.8 %collective-permute-done.23 = f32[4,64,512]{2,1,0:T(8,128)} collective-permute-done((f32[4,64,512]{2,1,0:T(8,128)}, f32[4,64,512]{2,1,0:T(8,128)}, u32[]{:S(2)}, u32[]{:S(2)}) %collective-permute-start.23) | collective-permute-done | bytes 524320 | tf_op jit(solution)/shard_map/ppermute | solution.py:12
  61.6 1.7 %fusion.11 = f32[32,512]{1,0:T(8,128)} fusion(f32[512,512]{1,0:T(8,128)S(1)} %bitcast.233, f32[32,512]{1,0:T(8,128)S(1)} %convolution_subtract_fusion.1, f32[32,512]{1,0:T(8,128)S(1)} %collective-permute-done.13), kind=kOutput, calls=%fused_computation.99 | convolution fusion | flops 100679680 | bytes 1245184 | tf_op jit(solution)/shard_map/dot_general | solution.py:59
  63.3 1.0 collective-permute-start.18
  65.5 6.0 %collective-permute-done.29 = f32[2,64,1024]{2,1,0:T(8,128)} collective-permute-done((f32[2,64,1024]{2,1,0:T(8,128)}, f32[2,64,1024]{2,1,0:T(8,128)}, u32[]{:S(2)}, u32[]{:S(2)}) %collective-permute-start.29) | collective-permute-done | bytes 524320 | tf_op jit(solution)/shard_map/ppermute | solution.py:12
  72.4 1.5 %select_bitcast_fusion.4 = f32[4,1,64,512]{3,2,1,0:T(8,128)S(1)} fusion(pred[]{:T(512)S(6)} %eq.223, f32[4,64,512]{2,1,0:T(8,128)} %collective-permute-done.22, pred[]{:T(512)S(6)} %eq.224, f32[4,64,512]{2,1,0:T(8,128)} %collective-permute-done.24, f32[4,64,512]{2,1,0:T(8,128)} %collective-permute-done.23, f32[1,64,512]{2,1,0:T(8,128)} %copy-done, ...), kind=kLoop, calls=%fused_computation.14 | loop fusion | flops 786432 | bytes 2621442 | tf_op jit(solution)/shard_map/stack | solution.py:22
  73.9 1.6 %select_bitcast_fusion.7 = (f32[4,1,64,512]{3,2,1,0:T(8,128)S(1)}, f32[4,1,64,512]{3,2,1,0:T(8,128)S(1)}, f32[4,1,64,512]{3,2,1,0:T(8,128)S(1)}) fusion(pred[]{:T(512)S(6)} %eq.223, f32[4,64,512]{2,1,0:T(8,128)} %collective-permute-done.22, pred[]{:T(512)S(6)} %eq.224, f32[4,64,512]{2,1,0:T(8,128)} %collective-permute-done.23, ...), kind=kLoop, calls=%fused_computation.17 | loop fusion | flops 1310720 | bytes 3670018 | tf_op jit(solution)/shard_map/stack | solution.py:22
  75.7 2.0 %convolution_subtract_fusion = f32[32,1024]{1,0:T(8,128)S(1)} fusion(f32[32,512]{1,0:T(8,128)S(1)} %add.282, f32[1024,512]{1,0:T(8,128)S(1)} %bitcast.229, f32[32,1024]{1,0:T(8,128)S(1)} %bitcast.239, pred[1024]{0:T(1024)(128)(4,1)S(1)} %broadcast_in_dim.87), kind=kOutput, calls=%fused_computation.2 | convolution fusion | flops 201392128 | bytes 2425856 | tf_op jit(solution)/shard_map/dot_general | solution.py:59
  77.8 1.0 collective-permute-start.25
  78.7 4.9 %collective-permute-done.25 = f32[32,1024]{1,0:T(8,128)S(1)} collective-permute-done((f32[32,1024]{1,0:T(8,128)S(1)}, f32[32,1024]{1,0:T(8,128)S(1)}, u32[]{:S(2)}, u32[]{:S(2)}) %collective-permute-start.25) | collective-permute-done | bytes 131104 | tf_op jit(solution)/shard_map/ppermute | solution.py:12
  83.6 2.0 %collective-permute-start.26 = (f32[32,1024]{1,0:T(8,128)S(1)}, f32[32,1024]{1,0:T(8,128)S(1)}, u32[]{:S(2)}, u32[]{:S(2)}) collective-permute-start(f32[32,1024]{1,0:T(8,128)S(1)} %add.290), channel_id=1, source_target_pairs={{0,16},{8,24},{16,0},{24,8},{1,17},{9,25},{17,1},{25,9},{2,18},{10... | collective-permute-start | bytes 393224 | tf_op jit(solution)/shard_map/ppermute | solution.py:12
  85.6 1.3 select_bitcast_fusion.3
  87.2 5.0 %collective-permute-done.26 = f32[32,1024]{1,0:T(8,128)S(1)} collective-permute-done((f32[32,1024]{1,0:T(8,128)S(1)}, f32[32,1024]{1,0:T(8,128)S(1)}, u32[]{:S(2)}, u32[]{:S(2)}) %collective-permute-start.26) | collective-permute-done | bytes 131104 | tf_op jit(solution)/shard_map/ppermute | solution.py:12
  92.3 2.0 %fusion = f32[32,512]{1,0:T(8,128)S(1)} fusion(f32[512,1024]{1,0:T(8,128)S(1)} %bitcast.231, f32[32,1024]{1,0:T(8,128)S(1)} %add.290, f32[32,1024]{1,0:T(8,128)S(1)} %collective-permute-done.26), kind=kOutput, calls=%fused_computation.52 | convolution fusion | flops 201359360 | bytes 2424832 | tf_op jit(solution)/shard_map/dot_general | solution.py:59
  94.3 1.0 collective-permute-start.31
  95.3 3.3 %collective-permute-done.31 = f32[32,512]{1,0:T(8,128)S(1)} collective-permute-done((f32[32,512]{1,0:T(8,128)S(1)}, f32[32,512]{1,0:T(8,128)S(1)}, u32[]{:S(2)}, u32[]{:S(2)}) %collective-permute-start.31) | collective-permute-done | bytes 65568 | tf_op jit(solution)/shard_map/ppermute | solution.py:12
  98.6 1.3 fusion.9
  100.0 5.0 %collective-permute-done.32 = f32[32,1024]{1,0:T(8,128)S(1)} collective-permute-done((f32[32,1024]{1,0:T(8,128)S(1)}, f32[32,1024]{1,0:T(8,128)S(1)}, u32[]{:S(2)}, u32[]{:S(2)}) %collective-permute-start.32) | collective-permute-done | bytes 131104 | tf_op jit(solution)/shard_map/ppermute | solution.py:12
  105.0 1.1 collective-permute-start.33
  106.1 5.8 %collective-permute-done.33 = f32[32,1024]{1,0:T(8,128)S(1)} collective-permute-done((f32[32,1024]{1,0:T(8,128)S(1)}, f32[32,1024]{1,0:T(8,128)S(1)}, u32[]{:S(2)}, u32[]{:S(2)}) %collective-permute-start.33) | collective-permute-done | bytes 131104 | tf_op jit(solution)/shard_map/ppermute | solution.py:12
  112.0 1.3 fusion.15
  113.3 1.0 collective-permute-start.34
  114.3 3.3 %collective-permute-done.34 = f32[32,512]{1,0:T(8,128)S(1)} collective-permute-done((f32[32,512]{1,0:T(8,128)S(1)}, f32[32,512]{1,0:T(8,128)S(1)}, u32[]{:S(2)}, u32[]{:S(2)}) %collective-permute-start.34) | collective-permute-done | bytes 65568 | tf_op jit(solution)/shard_map/ppermute | solution.py:12
  118.4 4.2 %collective-permute-done.35 = f32[32,512]{1,0:T(8,128)S(1)} collective-permute-done((f32[32,512]{1,0:T(8,128)S(1)}, f32[32,512]{1,0:T(8,128)S(1)}, u32[]{:S(2)}, u32[]{:S(2)}) %collective-permute-start.35) | collective-permute-done | bytes 65568 | tf_op jit(solution)/shard_map/ppermute | solution.py:12
  122.9 0.9 collective-permute-start.41
  123.8 1.0 collective-permute-start.42
  125.5 1.0 collective-permute-start.36
  127.3 2.6 %collective-permute-done.36 = f32[32,512]{1,0:T(8,128)S(1)} collective-permute-done((f32[32,512]{1,0:T(8,128)S(1)}, f32[32,512]{1,0:T(8,128)S(1)}, u32[]{:S(2)}, u32[]{:S(2)}) %collective-permute-start.36) | collective-permute-done | bytes 65568 | tf_op jit(solution)/shard_map/ppermute | solution.py:12
  131.3 1.0 collective-permute-start.39
  132.3 1.9 %collective-permute-done.38 = f32[1,32,64]{2,1,0:T(8,128)S(1)} collective-permute-done((f32[1,32,64]{2,1,0:T(8,128)S(1)}, f32[1,32,64]{2,1,0:T(8,128)S(1)}, u32[]{:S(2)}, u32[]{:S(2)}) %collective-permute-start.38) | collective-permute-done | bytes 8224 | tf_op jit(solution)/shard_map/ppermute | solution.py:12
  (161 shorter events, 20.1 us)
Async XLA Ops:
  0.0 10.3 %copy-start.9 = (f32[1,64,1024]{2,1,0:T(8,128)S(1)}, f32[1,64,1024]{2,1,0:T(8,128)}, u32[]{:S(2)}) copy-start(f32[1,64,1024]{2,1,0:T(8,128)} %param.12) | copy-start | bytes 786436
  0.0 10.4 %copy-start.7 = (f32[1,64,2048]{2,1,0:T(8,128)S(1)}, f32[1,64,2048]{2,1,0:T(8,128)}, u32[]{:S(2)}) copy-start(f32[1,64,2048]{2,1,0:T(8,128)} %param.13) | copy-start | bytes 1572868
  1.6 15.7 %collective-permute-start.3 = (f32[64,256]{1,0:T(8,128)}, f32[64,256]{1,0:T(8,128)S(1)}, u32[]{:S(2)}, u32[]{:S(2)}) collective-permute-start(f32[64,256]{1,0:T(8,128)} %dynamic-slice_bitcast_fusion.12), channel_id=1, source_target_pairs={{0,4},{1,5},{2,6},{3,7},{4,0},{5,1},{6,2},{7,3},{8,12},{9,13},{10,... | collective-permute-start | bytes 196616 | tf_op jit(solution)/shard_map/ppermute | solution.py:12
  4.6 16.3 %collective-permute-start.6 = (f32[64,256]{1,0:T(8,128)}, f32[64,256]{1,0:T(8,128)}, u32[]{:S(2)}, u32[]{:S(2)}) collective-permute-start(f32[64,256]{1,0:T(8,128)} %dynamic-slice_bitcast_fusion.12), channel_id=1, source_target_pairs={{0,6},{1,7},{2,4},{3,5},{4,2},{5,3},{6,0},{7,1},{8,14},{9,15},{10,... | collective-permute-start | bytes 196616 | tf_op jit(solution)/shard_map/ppermute | solution.py:12
  7.2 27.9 %collective-permute-start.27 = (f32[64,1024]{1,0:T(8,128)S(1)}, f32[64,1024]{1,0:T(8,128)S(1)}, u32[]{:S(2)}, u32[]{:S(2)}) collective-permute-start(f32[64,1024]{1,0:T(8,128)S(1)} %pad_maximum_fusion.10), channel_id=1, source_target_pairs={{0,4},{1,5},{2,6},{3,7},{4,0},{5,1},{6,2},{7,3},{8,12},{9,13},{10,... | collective-permute-start | bytes 786440 | tf_op jit(solution)/shard_map/ppermute | solution.py:12
  8.8 11.1 %copy-start.10 = (f32[1,64,512]{2,1,0:T(8,128)S(1)}, f32[1,64,512]{2,1,0:T(8,128)}, u32[]{:S(2)}) copy-start(f32[1,64,512]{2,1,0:T(8,128)} %param.9) | copy-start | bytes 393220
  9.1 3.6 %collective-permute-start.2 = (f32[3,32,64]{2,1,0:T(8,128)S(1)}, f32[3,32,64]{2,1,0:T(8,128)S(1)}, u32[]{:S(2)}, u32[]{:S(2)}) collective-permute-start(f32[3,32,64]{2,1,0:T(8,128)S(1)} %bitcast.247), channel_id=1, source_target_pairs={{0,3},{1,2},{2,1},{3,0},{4,7},{5,6},{6,5},{7,4},{8,11},{9,10},{10,... | collective-permute-start | bytes 73736 | tf_op jit(solution)/shard_map/ppermute | solution.py:12
  9.2 4.5 %collective-permute-start.1 = (f32[3,32,64]{2,1,0:T(8,128)S(1)}, f32[3,32,64]{2,1,0:T(8,128)S(1)}, u32[]{:S(2)}, u32[]{:S(2)}) collective-permute-start(f32[3,32,64]{2,1,0:T(8,128)S(1)} %bitcast.246), channel_id=1, source_target_pairs={{0,2},{1,3},{2,0},{3,1},{4,6},{5,7},{6,4},{7,5},{8,10},{9,11},{10,... | collective-permute-start | bytes 73736 | tf_op jit(solution)/shard_map/ppermute | solution.py:12
  12.6 7.4 %collective-permute-start.14 = (f32[64,512]{1,0:T(8,128)S(1)}, f32[64,512]{1,0:T(8,128)S(1)}, u32[]{:S(2)}, u32[]{:S(2)}) collective-permute-start(f32[64,512]{1,0:T(8,128)S(1)} %pad_maximum_fusion.14), channel_id=1, source_target_pairs={{0,4},{1,5},{2,6},{3,7},{4,0},{5,1},{6,2},{7,3},{8,12},{9,13},{10,... | collective-permute-start | bytes 393224 | tf_op jit(solution)/shard_map/ppermute | solution.py:12
  13.7 1.2 collective-permute-start
  14.9 10.7 %collective-permute-start.9 = (f32[64,512]{1,0:T(8,128)S(1)}, f32[64,512]{1,0:T(8,128)S(1)}, u32[]{:S(2)}, u32[]{:S(2)}) collective-permute-start(f32[64,512]{1,0:T(8,128)S(1)} %bitcast_multiply_fusion.4), channel_id=1, source_target_pairs={{0,8},{8,0},{16,24},{24,16},{1,9},{9,1},{17,25},{25,17},{2,10},{10... | collective-permute-start | bytes 393224 | tf_op jit(solution)/shard_map/ppermute | solution.py:12
  17.3 12.9 %collective-permute-start.20 = (f32[64,512]{1,0:T(8,128)S(1)}, f32[64,512]{1,0:T(8,128)S(1)}, u32[]{:S(2)}, u32[]{:S(2)}) collective-permute-start(f32[64,512]{1,0:T(8,128)S(1)} %get-tuple-element.32), channel_id=1, source_target_pairs={{0,16},{8,24},{16,0},{24,8},{1,17},{9,25},{17,1},{25,9},{2,18},{10... | collective-permute-start | bytes 393224 | tf_op jit(solution)/shard_map/ppermute | solution.py:12
  20.0 4.3 %collective-permute-start.5 = (f32[64,256]{1,0:T(8,128)S(1)}, f32[64,256]{1,0:T(8,128)S(1)}, u32[]{:S(2)}, u32[]{:S(2)}) collective-permute-start(f32[64,256]{1,0:T(8,128)S(1)} %get-tuple-element.10), channel_id=1, source_target_pairs={{0,2},{1,3},{2,0},{3,1},{4,6},{5,7},{6,4},{7,5},{8,10},{9,11},{10,... | collective-permute-start | bytes 196616 | tf_op jit(solution)/shard_map/ppermute | solution.py:12
  20.9 9.3 %collective-permute-start.21 = (f32[64,512]{1,0:T(8,128)S(1)}, f32[64,512]{1,0:T(8,128)S(1)}, u32[]{:S(2)}, u32[]{:S(2)}) collective-permute-start(f32[64,512]{1,0:T(8,128)S(1)} %get-tuple-element.31), channel_id=1, source_target_pairs={{0,24},{8,16},{16,8},{24,0},{1,25},{9,17},{17,9},{25,1},{2,26},{10... | collective-permute-start | bytes 393224 | tf_op jit(solution)/shard_map/ppermute | solution.py:12
  24.3 7.6 %collective-permute-start.19 = (f32[64,512]{1,0:T(8,128)S(1)}, f32[64,512]{1,0:T(8,128)S(1)}, u32[]{:S(2)}, u32[]{:S(2)}) collective-permute-start(f32[64,512]{1,0:T(8,128)S(1)} %get-tuple-element.30), channel_id=1, source_target_pairs={{0,8},{8,0},{16,24},{24,16},{1,9},{9,1},{17,25},{25,17},{2,10},{10... | collective-permute-start | bytes 393224 | tf_op jit(solution)/shard_map/ppermute | solution.py:12
  25.7 7.2 %collective-permute-start.4 = (f32[2,64,256]{2,1,0:T(8,128)S(1)}, f32[2,64,256]{2,1,0:T(8,128)S(1)}, u32[]{:S(2)}, u32[]{:S(2)}) collective-permute-start(f32[2,64,256]{2,1,0:T(8,128)S(1)} %pad_maximum_fusion.11), channel_id=1, source_target_pairs={{0,1},{1,0},{2,3},{3,2},{4,5},{5,4},{6,7},{7,6},{8,9},{9,8},{10,11... | collective-permute-start | bytes 393224 | tf_op jit(solution)/shard_map/ppermute | solution.py:12
  30.2 19.3 %collective-permute-start.15 = (f32[2,64,512]{2,1,0:T(8,128)S(1)}, f32[2,64,512]{2,1,0:T(8,128)S(1)}, u32[]{:S(2)}, u32[]{:S(2)}) collective-permute-start(f32[2,64,512]{2,1,0:T(8,128)S(1)} %pad_maximum_fusion.8), channel_id=1, source_target_pairs={{0,1},{1,0},{2,3},{3,2},{4,5},{5,4},{6,7},{7,6},{8,9},{9,8},{10,11... | collective-permute-start | bytes 786440 | tf_op jit(solution)/shard_map/ppermute | solution.py:12
  30.2 15.8 %collective-permute-start.16 = (f32[2,64,512]{2,1,0:T(8,128)S(1)}, f32[2,64,512]{2,1,0:T(8,128)S(1)}, u32[]{:S(2)}, u32[]{:S(2)}) collective-permute-start(f32[2,64,512]{2,1,0:T(8,128)S(1)} %pad_maximum_fusion.8), channel_id=1, source_target_pairs={{0,2},{1,3},{2,0},{3,1},{4,6},{5,7},{6,4},{7,5},{8,10},{9,11},{10,... | collective-permute-start | bytes 786440 | tf_op jit(solution)/shard_map/ppermute | solution.py:12
  31.9 1.5 %collective-permute-start.7 = (f32[2,64,256]{2,1,0:T(8,128)S(1)}, f32[2,64,256]{2,1,0:T(8,128)S(1)}, u32[]{:S(2)}, u32[]{:S(2)}) collective-permute-start(f32[2,64,256]{2,1,0:T(8,128)S(1)} %pad_maximum_fusion.12), channel_id=1, source_target_pairs={{0,1},{1,0},{2,3},{3,2},{4,5},{5,4},{6,7},{7,6},{8,9},{9,8},{10,11... | collective-permute-start | bytes 393224 | tf_op jit(solution)/shard_map/ppermute | solution.py:12
  32.9 14.1 %collective-permute-start.10 = (f32[2,64,512]{2,1,0:T(8,128)S(1)}, f32[2,64,512]{2,1,0:T(8,128)S(1)}, u32[]{:S(2)}, u32[]{:S(2)}) collective-permute-start(f32[2,64,512]{2,1,0:T(8,128)S(1)} %pad_maximum_fusion.7), channel_id=1, source_target_pairs={{0,1},{1,0},{2,3},{3,2},{4,5},{5,4},{6,7},{7,6},{8,9},{9,8},{10,11... | collective-permute-start | bytes 786440 | tf_op jit(solution)/shard_map/ppermute | solution.py:12
  33.4 11.2 %collective-permute-start.11 = (f32[2,64,512]{2,1,0:T(8,128)S(1)}, f32[2,64,512]{2,1,0:T(8,128)S(1)}, u32[]{:S(2)}, u32[]{:S(2)}) collective-permute-start(f32[2,64,512]{2,1,0:T(8,128)S(1)} %pad_maximum_fusion.7), channel_id=1, source_target_pairs={{0,2},{1,3},{2,0},{3,1},{4,6},{5,7},{6,4},{7,5},{8,10},{9,11},{10,... | collective-permute-start | bytes 786440 | tf_op jit(solution)/shard_map/ppermute | solution.py:12
  35.1 10.4 %collective-permute-start.8 = (f32[32,512]{1,0:T(8,128)S(1)}, f32[32,512]{1,0:T(8,128)S(1)}, u32[]{:S(2)}, u32[]{:S(2)}) collective-permute-start(f32[32,512]{1,0:T(8,128)S(1)} %fusion.14), channel_id=1, source_target_pairs={{0,4},{1,5},{2,6},{3,7},{4,0},{5,1},{6,2},{7,3},{8,12},{9,13},{10,... | collective-permute-start | bytes 196616 | tf_op jit(solution)/shard_map/ppermute | solution.py:12
  44.6 3.6 %collective-permute-start.12 = (f32[2,64,512]{2,1,0:T(8,128)S(1)}, f32[2,64,512]{2,1,0:T(8,128)S(1)}, u32[]{:S(2)}, u32[]{:S(2)}) collective-permute-start(f32[2,64,512]{2,1,0:T(8,128)S(1)} %collective-permute-done.11), channel_id=1, source_target_pairs={{0,1},{1,0},{2,3},{3,2},{4,5},{5,4},{6,7},{7,6},{8,9},{9,8},{10,11... | collective-permute-start | bytes 786440 | tf_op jit(solution)/shard_map/ppermute | solution.py:12
  45.5 26.9 %collective-permute-start.22 = (f32[4,64,512]{2,1,0:T(8,128)}, f32[4,64,512]{2,1,0:T(8,128)}, u32[]{:S(2)}, u32[]{:S(2)}) collective-permute-start(f32[4,64,512]{2,1,0:T(8,128)} %pad_maximum_fusion.5), channel_id=1, source_target_pairs={{0,1},{1,0},{2,3},{3,2},{4,5},{5,4},{6,7},{7,6},{8,9},{9,8},{10,11... | collective-permute-start | bytes 1572872 | tf_op jit(solution)/shard_map/ppermute | solution.py:12
  46.0 15.2 %collective-permute-start.23 = (f32[4,64,512]{2,1,0:T(8,128)}, f32[4,64,512]{2,1,0:T(8,128)}, u32[]{:S(2)}, u32[]{:S(2)}) collective-permute-start(f32[4,64,512]{2,1,0:T(8,128)} %pad_maximum_fusion.5), channel_id=1, source_target_pairs={{0,2},{1,3},{2,0},{3,1},{4,6},{5,7},{6,4},{7,5},{8,10},{9,11},{10,... | collective-permute-start | bytes 1572872 | tf_op jit(solution)/shard_map/ppermute | solution.py:12
  47.0 24.5 %collective-permute-start.29 = (f32[2,64,1024]{2,1,0:T(8,128)}, f32[2,64,1024]{2,1,0:T(8,128)}, u32[]{:S(2)}, u32[]{:S(2)}) collective-permute-start(f32[2,64,1024]{2,1,0:T(8,128)} %pad_maximum_fusion.6), channel_id=1, source_target_pairs={{0,2},{1,3},{2,0},{3,1},{4,6},{5,7},{6,4},{7,5},{8,10},{9,11},{10,... | collective-permute-start | bytes 1572872 | tf_op jit(solution)/shard_map/ppermute | solution.py:12
  48.1 13.1 %collective-permute-start.17 = (f32[2,64,512]{2,1,0:T(8,128)S(1)}, f32[2,64,512]{2,1,0:T(8,128)S(1)}, u32[]{:S(2)}, u32[]{:S(2)}) collective-permute-start(f32[2,64,512]{2,1,0:T(8,128)S(1)} %collective-permute-done.16), channel_id=1, source_target_pairs={{0,1},{1,0},{2,3},{3,2},{4,5},{5,4},{6,7},{7,6},{8,9},{9,8},{10,11... | collective-permute-start | bytes 786440 | tf_op jit(solution)/shard_map/ppermute | solution.py:12
  49.5 12.1 %collective-permute-start.13 = (f32[32,512]{1,0:T(8,128)S(1)}, f32[32,512]{1,0:T(8,128)S(1)}, u32[]{:S(2)}, u32[]{:S(2)}) collective-permute-start(f32[32,512]{1,0:T(8,128)S(1)} %convolution_subtract_fusion.1), channel_id=1, source_target_pairs={{0,8},{8,0},{16,24},{24,16},{1,9},{9,1},{17,25},{25,17},{2,10},{10... | collective-permute-start | bytes 196616 | tf_op jit(solution)/shard_map/ppermute | solution.py:12
  61.2 11.2 %collective-permute-start.24 = (f32[4,64,512]{2,1,0:T(8,128)}, f32[4,64,512]{2,1,0:T(8,128)}, u32[]{:S(2)}, u32[]{:S(2)}) collective-permute-start(f32[4,64,512]{2,1,0:T(8,128)} %collective-permute-done.23), channel_id=1, source_target_pairs={{0,1},{1,0},{2,3},{3,2},{4,5},{5,4},{6,7},{7,6},{8,9},{9,8},{10,11... | collective-permute-start | bytes 1572872 | tf_op jit(solution)/shard_map/ppermute | solution.py:12
  63.3 8.2 %collective-permute-start.18 = (f32[32,512]{1,0:T(8,128)}, f32[32,512]{1,0:T(8,128)}, u32[]{:S(2)}, u32[]{:S(2)}) collective-permute-start(f32[32,512]{1,0:T(8,128)} %fusion.11), channel_id=1, source_target_pairs={{0,4},{1,5},{2,6},{3,7},{4,0},{5,1},{6,2},{7,3},{8,12},{9,13},{10,... | collective-permute-start | bytes 196616 | tf_op jit(solution)/shard_map/ppermute | solution.py:12
  65.2 20.4 %collective-permute-start.28 = (f32[2,64,1024]{2,1,0:T(8,128)}, f32[2,64,1024]{2,1,0:T(8,128)S(1)}, u32[]{:S(2)}, u32[]{:S(2)}) collective-permute-start(f32[2,64,1024]{2,1,0:T(8,128)} %pad_maximum_fusion.6), channel_id=1, source_target_pairs={{0,1},{1,0},{2,3},{3,2},{4,5},{5,4},{6,7},{7,6},{8,9},{9,8},{10,11... | collective-permute-start | bytes 1572872 | tf_op jit(solution)/shard_map/ppermute | solution.py:12
  71.5 14.2 %collective-permute-start.30 = (f32[2,64,1024]{2,1,0:T(8,128)}, f32[2,64,1024]{2,1,0:T(8,128)S(1)}, u32[]{:S(2)}, u32[]{:S(2)}) collective-permute-start(f32[2,64,1024]{2,1,0:T(8,128)} %collective-permute-done.29), channel_id=1, source_target_pairs={{0,1},{1,0},{2,3},{3,2},{4,5},{5,4},{6,7},{7,6},{8,9},{9,8},{10,11... | collective-permute-start | bytes 1572872 | tf_op jit(solution)/shard_map/ppermute | solution.py:12
  77.8 5.8 %collective-permute-start.25 = (f32[32,1024]{1,0:T(8,128)S(1)}, f32[32,1024]{1,0:T(8,128)S(1)}, u32[]{:S(2)}, u32[]{:S(2)}) collective-permute-start(f32[32,1024]{1,0:T(8,128)S(1)} %convolution_subtract_fusion), channel_id=1, source_target_pairs={{0,8},{8,0},{16,24},{24,16},{1,9},{9,1},{17,25},{25,17},{2,10},{10... | collective-permute-start | bytes 393224 | tf_op jit(solution)/shard_map/ppermute | solution.py:12
  83.6 8.7 %collective-permute-start.26 = (f32[32,1024]{1,0:T(8,128)S(1)}, f32[32,1024]{1,0:T(8,128)S(1)}, u32[]{:S(2)}, u32[]{:S(2)}) collective-permute-start(f32[32,1024]{1,0:T(8,128)S(1)} %add.290), channel_id=1, source_target_pairs={{0,16},{8,24},{16,0},{24,8},{1,17},{9,25},{17,1},{25,9},{2,18},{10... | collective-permute-start | bytes 393224 | tf_op jit(solution)/shard_map/ppermute | solution.py:12
  94.3 4.3 %collective-permute-start.31 = (f32[32,512]{1,0:T(8,128)S(1)}, f32[32,512]{1,0:T(8,128)S(1)}, u32[]{:S(2)}, u32[]{:S(2)}) collective-permute-start(f32[32,512]{1,0:T(8,128)S(1)} %fusion), channel_id=1, source_target_pairs={{0,4},{1,5},{2,6},{3,7},{4,0},{5,1},{6,2},{7,3},{8,12},{9,13},{10,... | collective-permute-start | bytes 196616 | tf_op jit(solution)/shard_map/ppermute | solution.py:12
  99.9 17.7 %copy-start.6 = (f32[32,512]{1,0:T(8,128)S(1)}, f32[32,512]{1,0:T(8,128)}, u32[]{:S(2)}) copy-start(f32[32,512]{1,0:T(8,128)} %copy-done.5) | copy-start | bytes 196612
  99.9 5.0 %collective-permute-start.32 = (f32[32,1024]{1,0:T(8,128)S(1)}, f32[32,1024]{1,0:T(8,128)S(1)}, u32[]{:S(2)}, u32[]{:S(2)}) collective-permute-start(f32[32,1024]{1,0:T(8,128)S(1)} %fusion.9), channel_id=1, source_target_pairs={{0,8},{8,0},{16,24},{24,16},{1,9},{9,1},{17,25},{25,17},{2,10},{10... | collective-permute-start | bytes 393224 | tf_op jit(solution)/shard_map/ppermute | solution.py:12
  105.0 6.9 %collective-permute-start.33 = (f32[32,1024]{1,0:T(8,128)S(1)}, f32[32,1024]{1,0:T(8,128)S(1)}, u32[]{:S(2)}, u32[]{:S(2)}) collective-permute-start(f32[32,1024]{1,0:T(8,128)S(1)} %add.305), channel_id=1, source_target_pairs={{0,16},{8,24},{16,0},{24,8},{1,17},{9,25},{17,1},{25,9},{2,18},{10... | collective-permute-start | bytes 393224 | tf_op jit(solution)/shard_map/ppermute | solution.py:12
  113.3 16.6 %copy-start.4 = (f32[32,512]{1,0:T(8,128)S(1)}, f32[32,512]{1,0:T(8,128)}, u32[]{:S(2)}) copy-start(f32[32,512]{1,0:T(8,128)} %copy-done.3) | copy-start | bytes 196612
  113.3 4.3 %collective-permute-start.34 = (f32[32,512]{1,0:T(8,128)S(1)}, f32[32,512]{1,0:T(8,128)S(1)}, u32[]{:S(2)}, u32[]{:S(2)}) collective-permute-start(f32[32,512]{1,0:T(8,128)S(1)} %fusion.15), channel_id=1, source_target_pairs={{0,4},{1,5},{2,6},{3,7},{4,0},{5,1},{6,2},{7,3},{8,12},{9,13},{10,... | collective-permute-start | bytes 196616 | tf_op jit(solution)/shard_map/ppermute | solution.py:12
  118.3 4.3 %collective-permute-start.35 = (f32[32,512]{1,0:T(8,128)S(1)}, f32[32,512]{1,0:T(8,128)S(1)}, u32[]{:S(2)}, u32[]{:S(2)}) collective-permute-start(f32[32,512]{1,0:T(8,128)S(1)} %fusion.6), channel_id=1, source_target_pairs={{0,8},{8,0},{16,24},{24,16},{1,9},{9,1},{17,25},{25,17},{2,10},{10... | collective-permute-start | bytes 196616 | tf_op jit(solution)/shard_map/ppermute | solution.py:12
  122.8 3.7 %collective-permute-start.40 = (f32[2,32,64]{2,1,0:T(8,128)S(1)}, f32[2,32,64]{2,1,0:T(8,128)S(1)}, u32[]{:S(2)}, u32[]{:S(2)}) collective-permute-start(f32[2,32,64]{2,1,0:T(8,128)S(1)} %slice_select_fusion.2), channel_id=1, source_target_pairs={{0,1},{1,0},{2,3},{3,2},{4,5},{5,4},{6,7},{7,6},{8,9},{9,8},{10,11... | collective-permute-start | bytes 49160 | tf_op jit(solution)/shard_map/ppermute | solution.py:12
  122.9 4.0 %collective-permute-start.41 = (f32[2,32,64]{2,1,0:T(8,128)S(1)}, f32[2,32,64]{2,1,0:T(8,128)S(1)}, u32[]{:S(2)}, u32[]{:S(2)}) collective-permute-start(f32[2,32,64]{2,1,0:T(8,128)S(1)} %get-tuple-element.73), channel_id=1, source_target_pairs={{0,2},{1,3},{2,0},{3,1},{4,6},{5,7},{6,4},{7,5},{8,10},{9,11},{10,... | collective-permute-start | bytes 49160 | tf_op jit(solution)/shard_map/ppermute | solution.py:12
  123.8 3.4 %collective-permute-start.42 = (f32[2,32,64]{2,1,0:T(8,128)S(1)}, f32[2,32,64]{2,1,0:T(8,128)S(1)}, u32[]{:S(2)}, u32[]{:S(2)}) collective-permute-start(f32[2,32,64]{2,1,0:T(8,128)S(1)} %get-tuple-element.72), channel_id=1, source_target_pairs={{0,3},{1,2},{2,1},{3,0},{4,7},{5,6},{6,5},{7,4},{8,11},{9,10},{10,... | collective-permute-start | bytes 49160 | tf_op jit(solution)/shard_map/ppermute | solution.py:12
  125.5 4.4 %collective-permute-start.36 = (f32[32,512]{1,0:T(8,128)S(1)}, f32[32,512]{1,0:T(8,128)S(1)}, u32[]{:S(2)}, u32[]{:S(2)}) collective-permute-start(f32[32,512]{1,0:T(8,128)S(1)} %fusion.16), channel_id=1, source_target_pairs={{0,4},{1,5},{2,6},{3,7},{4,0},{5,1},{6,2},{7,3},{8,12},{9,13},{10,... | collective-permute-start | bytes 196616 | tf_op jit(solution)/shard_map/ppermute | solution.py:12
  130.3 2.0 %collective-permute-start.37 = (f32[1,32,64]{2,1,0:T(8,128)S(1)}, f32[1,32,64]{2,1,0:T(8,128)S(1)}, u32[]{:S(2)}, u32[]{:S(2)}) collective-permute-start(f32[1,32,64]{2,1,0:T(8,128)S(1)} %slice_select_fusion.6), channel_id=1, source_target_pairs={{0,1},{1,0},{2,3},{3,2},{4,5},{5,4},{6,7},{7,6},{8,9},{9,8},{10,11... | collective-permute-start | bytes 24584 | tf_op jit(solution)/shard_map/ppermute | solution.py:12
  130.4 3.7 %collective-permute-start.38 = (f32[1,32,64]{2,1,0:T(8,128)S(1)}, f32[1,32,64]{2,1,0:T(8,128)S(1)}, u32[]{:S(2)}, u32[]{:S(2)}) collective-permute-start(f32[1,32,64]{2,1,0:T(8,128)S(1)} %get-tuple-element.75), channel_id=1, source_target_pairs={{0,2},{1,3},{2,0},{3,1},{4,6},{5,7},{6,4},{7,5},{8,10},{9,11},{10,... | collective-permute-start | bytes 24584 | tf_op jit(solution)/shard_map/ppermute | solution.py:12
  131.3 3.2 %collective-permute-start.39 = (f32[1,32,64]{2,1,0:T(8,128)S(1)}, f32[1,32,64]{2,1,0:T(8,128)S(1)}, u32[]{:S(2)}, u32[]{:S(2)}) collective-permute-start(f32[1,32,64]{2,1,0:T(8,128)S(1)} %get-tuple-element.74), channel_id=1, source_target_pairs={{0,3},{1,2},{2,1},{3,0},{4,7},{5,6},{6,5},{7,4},{8,11},{9,10},{10,... | collective-permute-start | bytes 24584 | tf_op jit(solution)/shard_map/ppermute | solution.py:12
  (8 other events, 56.7 us)
where the time goes:
time: 136 us; the launch traced here: 135 us
  waiting for transfers between devices  71.9 us (53%)
  starting transfers between devices  34.4 us (25%)
  matrix products  11.7 us (9%)
  other arithmetic  10.1 us (7%)
  local copies, waits for them, and re-layouts  6.43 us (5%)
    ppermute x43, waiting for transfers between devices, exchange(): return lax.ppermute(value, axis, pairs)  71.9 us
    ppermute x43, starting transfers between devices, exchange(): return lax.ppermute(value, axis, pairs)  34.4 us
    dot_general x10, matrix products, times(): lax.dot_general(vector, matrix, (((1,), (contract,)), ((), ())), precisio...  11.7 us
    another operation x31, other arithmetic, absolute(): return jnp.stack(pieces, axis)  8.49 us
  transfers between devices with their start and end apart: 43, of which 21 were waited for; matrix products, arithmetic and copies ran while one was open for 15% of the time, Pallas kernels for 0%

commit v1 on v0

--- a/solution.py
+++ b/solution.py
@@ -13,13 +13,21 @@
 
 
 def absolute(pieces, index, axis=0):
-    count, bit = len(pieces), 1
-    while bit < count:
-        pieces = [
-            jnp.where(index // bit % 2 == 0, pieces[m], pieces[m ^ bit]) for m in range(count)
-        ]
-        bit *= 2
-    return jnp.stack(pieces, axis)
+    if len(pieces) == 1:
+        return jnp.expand_dims(pieces[0], axis)
+    if len(pieces) == 2:
+        return jnp.where(
+            index % 2 == 0, jnp.stack(pieces, axis), jnp.stack(pieces[::-1], axis)
+        )
+    half = len(pieces) // 2
+    first, second = (
+        absolute(part, index % half, axis) for part in (pieces[:half], pieces[half:])
+    )
+    return jnp.where(
+        index // half == 0,
+        jnp.concatenate([first, second], axis),
+        jnp.concatenate([second, first], axis),
+    )
 
 
 def team_order(pieces, g):
@@ -50,7 +58,8 @@
 def summed(value, axis, count, unit):
     bit = 1
     while bit < count:
-        value = value + exchange(value, axis, bit * unit)
+        mask = 2 * bit - 1 if axis == "cube" else bit * unit
+        value = value + exchange(value, axis, mask)
         bit *= 2
     return value
 
@@ -80,7 +89,18 @@
     width, half, full = columns // TEAM, TEAM * rows, front * rows
     group_mid, group_top = inverse_mid.shape[2] // full, inverse_top.shape[2] // full
 
-    def inverse_pieces(inverse, count):
+    def whole_block(own, across):
+        if across is None:
+            across = exchange(own, "front", 2)
+        beside = exchange(own, "front", 1)
+        both = exchange(across, "front", 1)
+        count, _, wide = own.shape
+        whole = jnp.zeros((count, TEAM, rows, wide), jnp.float32)
+        for m, piece in ((0, own), (1, beside), (2, across), (3, both)):
+            whole = lax.dynamic_update_slice(whole, piece[:, None], (0, g ^ m, 0, 0))
+        return whole.reshape(-1, wide)
+
+    def part_pieces(inverse, count):
         return [
             jnp.concatenate([
                 lax.dynamic_slice_in_dim(inverse[0], (block * parts + (q ^ m)) * half, half, 1)
@@ -89,32 +109,28 @@
             for m in range(parts)
         ]
 
-    def coupling_pieces(coupling, pattern, count):
-        keep = jnp.repeat(pattern[0].astype(jnp.float32), TILE, axis=1)
-        starts = [(cube_pos % count ^ m) * full for m in range(count)]
+    def in_order(pieces):
+        return absolute(pieces, q)
+
+    def inverse_block(inverse, count):
+        pieces = to_parts(part_pieces(inverse, count), "front", TEAM)
+        return whole_block(in_order(pieces), None)
+
+    def with_cube(coupling, keep, count):
+        pieces = [
+            lax.dynamic_slice_in_dim(coupling[0], (cube_pos % count ^ m) * full, full, 1)
+            * keep[m : m + 1]
+            for m in range(count)
+        ]
+        pieces = to_parts(pieces, "cube", 1)
+        return absolute(pieces, cube_pos % count)
+
+    def present(tiles, start, count):
+        wide = front * rows // TILE
         return [
-            lax.dynamic_slice_in_dim(coupling[0], start, full, 1)
-            * lax.dynamic_slice_in_dim(keep, start, full, 1)
-            for start in starts
+            lax.dynamic_slice_in_dim(tiles, start + (cube_pos % count ^ m) * wide, wide, 1)
+            for m in range(count)
         ]
-
-    def whole_block(own, across):
-        if across is None:
-            across = exchange(own, "front", 2)
-        beside = exchange(own, "front", 1)
-        both = exchange(across, "front", 1)
-        whole = absolute([own, beside, across, both], g, axis=1)
-        return whole.reshape(TEAM * own.shape[0] * rows, own.shape[2])
-
-    def inverse_block(inverse, count):
-        pieces = inverse_pieces(inverse, count)
-        own = absolute(to_parts(pieces, "front", TEAM), q)
-        return whole_block(own, None)
-
-    def coupling_block(coupling, pattern, count):
-        pieces = coupling_pieces(coupling, pattern, count)
-        own = absolute(to_parts(pieces, "cube", 1), cube_pos % count)
-        return whole_block(own, None)
 
     def own_rows(side, count):
         here = lax.broadcasted_iota(jnp.int32, (1, count, 1), 1) == cube_pos % count
@@ -128,18 +144,26 @@
         turned = absolute(pieces, g, axis=1).reshape(value.shape[0], columns, rows)
         return jnp.swapaxes(turned, 1, 2)
 
-    pieces = inverse_pieces(inverse_leaf, 1)
-    own = absolute(to_parts(pieces, "front", TEAM), q)
-    across = absolute([exchange(piece, "front", m * TEAM + 2) for m, piece in enumerate(pieces)], q)
     turned = jnp.swapaxes(right_sides[:, 0], 1, 2)
     sides = team_order(to_parts([
         lax.dynamic_slice_in_dim(turned, (g ^ m) * width, width, 1) for m in range(TEAM)
     ], "front", 1), g)
 
+    pieces = part_pieces(inverse_leaf, 1)
+    own = in_order(to_parts(pieces, "front", TEAM))
+    across = in_order([exchange(piece, "front", m * TEAM + 2) for m, piece in enumerate(pieces)])
     leaf = whole_block(own, across)
-    couple_mid = coupling_block(coupling_mid, pattern_mid, group_mid)
+    both = jnp.concatenate([pattern_mid[0], pattern_top[0]], axis=1)
+    tiles = present(both, 0, group_mid) + present(both, pattern_mid.shape[2], group_top)
+    wide = front * rows // TILE
+    spread = lax.broadcasted_iota(jnp.int32, (wide, full), 1) // TILE
+    spread = spread == lax.broadcasted_iota(jnp.int32, (wide, full), 0)
+    keep = times(jnp.concatenate(tiles).astype(jnp.float32), spread.astype(jnp.float32), 0)
+    couple_mid = with_cube(coupling_mid, keep[:group_mid], group_mid)
+    couple_mid = whole_block(couple_mid, None)
     mid = inverse_block(inverse_mid, group_mid)
-    couple_top = coupling_block(coupling_top, pattern_top, group_top)
+    couple_top = with_cube(coupling_top, keep[group_mid:], group_top)
+    couple_top = whole_block(couple_top, None)
     top = inverse_block(inverse_top, group_top)
 
     y0 = summed(times(sides[0], leaf, 1), "front", parts, TEAM)

time: 136 us -> 131 us (0.963)
  other arithmetic: 10.1 us -> 3.36 us
  starting transfers between devices: 34.4 us -> 40.1 us
  waiting for transfers between devices: 71.9 us -> 69.6 us
    another operation x31 -> x5, other arithmetic: 8.49 us -> 0.88 us  [absolute(): jnp.stack(pieces, axis)]
    ppermute x43, starting transfers between devices: 34.4 us -> 40.1 us  [exchange(): return lax.ppermute(value, axis, pairs)]
    ppermute x43, waiting for transfers between devices: 71.9 us -> 69.6 us  [exchange(): return lax.ppermute(value, axis, pairs)]
    broadcast_in_dim x7, local copies, waits for them, and re-layouts: 1.64 us -> 0.24 us  [own_rows(): return jnp.where(here, side[:, None], 0.0).reshape(width, count * half)]
    dynamic_slice x5 -> x4, local copies, waits for them, and re-layouts: 2.72 us -> 2.18 us  [the longest x3 2.1 us: part_pieces(): lax.dynamic_slice_in_dim(inverse[0], (block * parts + (q ^ m)) * half, ha...]
    dot_general x10 -> x11, matrix products: 11.7 us -> 11.3 us  [times(): lax.dot_general(vector, matrix, (((1,), (contract,)), ((), ())), precisio...]
  transfers between devices with their start and end apart: 43 -> 43, of which waited for: 21 -> 22; matrix products, arithmetic and copies ran while one was open for 15% -> 8% of each run, Pallas kernels for 0% -> 0%
where the time goes in v1:
time: 131 us
  waiting for transfers between devices  69.6 us (53%)
  starting transfers between devices  40.1 us (31%)
  matrix products  11.3 us (9%)
  local copies, waits for them, and re-layouts  5.35 us (4%)
  other arithmetic  3.36 us (3%)
    ppermute x43, waiting for transfers between devices, exchange(): return lax.ppermute(value, axis, pairs)  69.6 us
    ppermute x43, starting transfers between devices, exchange(): return lax.ppermute(value, axis, pairs)  40.1 us
    dot_general x11, matrix products, times(): lax.dot_general(vector, matrix, (((1,), (contract,)), ((), ())), precisio...  11.3 us
  transfers between devices with their start and end apart: 43, of which 22 were waited for; matrix products, arithmetic and copies ran while one was open for 8% of the time, Pallas kernels for 0%

profile of v1, /device:TPU:0, one launch (start us, length us, event | category | flops | bytes accessed | tf_op | source)
XLA Modules:
  0.0 130.9 jit_solution(14073166007613339942)
XLA Ops:
  0.0 1.0 constant_dynamic-slice_fusion.6
  1.0 3.1 %collective-permute-start.3 = (f32[64,256]{1,0:T(8,128)S(1)}, f32[64,256]{1,0:T(8,128)S(1)}, u32[]{:S(2)}, u32[]{:S(2)}) collective-permute-start(f32[64,256]{1,0:T(8,128)S(1)} %get-tuple-element.23), channel_id=1, source_target_pairs={{0,4},{1,5},{2,6},{3,7},{4,0},{5,1},{6,2},{7,3},{8,12},{9,13},{10,... | collective-permute-start | bytes 196616 | tf_op jit(solution)/shard_map/ppermute | solution.py:12
  4.1 1.4 %collective-permute-start.6 = (f32[64,256]{1,0:T(8,128)S(1)}, f32[64,256]{1,0:T(8,128)S(1)}, u32[]{:S(2)}, u32[]{:S(2)}) collective-permute-start(f32[64,256]{1,0:T(8,128)S(1)} %get-tuple-element.23), channel_id=1, source_target_pairs={{0,6},{1,7},{2,4},{3,5},{4,2},{5,3},{6,0},{7,1},{8,14},{9,15},{10,... | collective-permute-start | bytes 196616 | tf_op jit(solution)/shard_map/ppermute | solution.py:12
  5.5 1.1 dynamic-slice_bitcast_fusion.7
  6.7 0.7 pad_maximum_fusion.1
  7.4 1.5 %collective-permute-start.27 = (f32[64,1024]{1,0:T(8,128)}, f32[64,1024]{1,0:T(8,128)S(1)}, u32[]{:S(2)}, u32[]{:S(2)}) collective-permute-start(f32[64,1024]{1,0:T(8,128)} %pad_maximum_fusion.1), channel_id=1, source_target_pairs={{0,4},{1,5},{2,6},{3,7},{4,0},{5,1},{6,2},{7,3},{8,12},{9,13},{10,... | collective-permute-start | bytes 786440 | tf_op jit(solution)/shard_map/ppermute | solution.py:12
  14.2 0.8 collective-permute-done
  15.0 0.8 collective-permute-start.5
  16.1 1.6 %collective-permute-start.9 = (f32[64,512]{1,0:T(8,128)}, f32[64,512]{1,0:T(8,128)S(1)}, u32[]{:S(2)}, u32[]{:S(2)}) collective-permute-start(f32[64,512]{1,0:T(8,128)} %bitcast_multiply_fusion.3), channel_id=1, source_target_pairs={{0,8},{8,0},{16,24},{24,16},{1,9},{9,1},{17,25},{25,17},{2,10},{10... | collective-permute-start | bytes 393224 | tf_op jit(solution)/shard_map/ppermute | solution.py:12
  17.8 2.7 %collective-permute-start.20 = (f32[64,512]{1,0:T(8,128)S(1)}, f32[64,512]{1,0:T(8,128)S(1)}, u32[]{:S(2)}, u32[]{:S(2)}) collective-permute-start(f32[64,512]{1,0:T(8,128)S(1)} %get-tuple-element.7), channel_id=1, source_target_pairs={{0,16},{8,24},{16,0},{24,8},{1,17},{9,25},{17,1},{25,9},{2,18},{10... | collective-permute-start | bytes 393224 | tf_op jit(solution)/shard_map/ppermute | solution.py:12
  20.4 2.5 %collective-permute-start.21 = (f32[64,512]{1,0:T(8,128)S(1)}, f32[64,512]{1,0:T(8,128)S(1)}, u32[]{:S(2)}, u32[]{:S(2)}) collective-permute-start(f32[64,512]{1,0:T(8,128)S(1)} %get-tuple-element.6), channel_id=1, source_target_pairs={{0,24},{8,16},{16,8},{24,0},{1,25},{9,17},{17,9},{25,1},{2,26},{10... | collective-permute-start | bytes 393224 | tf_op jit(solution)/shard_map/ppermute | solution.py:12
  23.0 7.8 %collective-permute-done.20 = f32[64,512]{1,0:T(8,128)S(1)} collective-permute-done((f32[64,512]{1,0:T(8,128)S(1)}, f32[64,512]{1,0:T(8,128)S(1)}, u32[]{:S(2)}, u32[]{:S(2)}) %collective-permute-start.20) | collective-permute-done | bytes 131104 | tf_op jit(solution)/shard_map/ppermute | solution.py:12
  30.9 4.9 %collective-permute-done.19 = f32[64,512]{1,0:T(8,128)S(1)} collective-permute-done((f32[64,512]{1,0:T(8,128)S(1)}, f32[64,512]{1,0:T(8,128)S(1)}, u32[]{:S(2)}, u32[]{:S(2)}) %collective-permute-start.19) | collective-permute-done | bytes 131104 | tf_op jit(solution)/shard_map/ppermute | solution.py:12
  36.6 1.3 collective-permute-start.16
  38.9 0.9 collective-permute-start.11
  40.4 1.5 %collective-permute-start.8 = (f32[32,512]{1,0:T(8,128)S(1)}, f32[32,512]{1,0:T(8,128)S(1)}, u32[]{:S(2)}, u32[]{:S(2)}) collective-permute-start(f32[32,512]{1,0:T(8,128)S(1)} %fusion.23), channel_id=1, source_target_pairs={{0,4},{1,5},{2,6},{3,7},{4,0},{5,1},{6,2},{7,3},{8,12},{9,13},{10,... | collective-permute-start | bytes 196616 | tf_op jit(solution)/shard_map/ppermute | solution.py:12
  42.2 2.5 %collective-permute-done.8 = f32[32,512]{1,0:T(8,128)S(1)} collective-permute-done((f32[32,512]{1,0:T(8,128)S(1)}, f32[32,512]{1,0:T(8,128)S(1)}, u32[]{:S(2)}, u32[]{:S(2)}) %collective-permute-start.8) | collective-permute-done | bytes 65568 | tf_op jit(solution)/shard_map/ppermute | solution.py:12
  44.8 1.3 collective-permute-start.23
  46.1 5.4 %collective-permute-done.11 = f32[2,64,512]{2,1,0:T(8,128)S(1)} collective-permute-done((f32[2,64,512]{2,1,0:T(8,128)S(1)}, f32[2,64,512]{2,1,0:T(8,128)S(1)}, u32[]{:S(2)}, u32[]{:S(2)}) %collective-permute-start.11) | collective-permute-done | bytes 262176 | tf_op jit(solution)/shard_map/ppermute | solution.py:12
  52.1 1.3 collective-permute-start.29
  53.9 1.0 convolution_subtract_fusion.1
  55.0 7.6 %collective-permute-done.23 = f32[4,64,512]{2,1,0:T(8,128)S(1)} collective-permute-done((f32[4,64,512]{2,1,0:T(8,128)S(1)}, f32[4,64,512]{2,1,0:T(8,128)S(1)}, u32[]{:S(2)}, u32[]{:S(2)}) %collective-permute-start.23) | collective-permute-done | bytes 524320 | tf_op jit(solution)/shard_map/ppermute | solution.py:12
  62.8 1.0 fusion.20
  63.8 1.5 %collective-permute-start.18 = (f32[32,512]{1,0:T(8,128)S(1)}, f32[32,512]{1,0:T(8,128)S(1)}, u32[]{:S(2)}, u32[]{:S(2)}) collective-permute-start(f32[32,512]{1,0:T(8,128)S(1)} %fusion.20), channel_id=1, source_target_pairs={{0,4},{1,5},{2,6},{3,7},{4,0},{5,1},{6,2},{7,3},{8,12},{9,13},{10,... | collective-permute-start | bytes 196616 | tf_op jit(solution)/shard_map/ppermute | solution.py:12
  65.4 7.6 %collective-permute-done.29 = f32[2,64,1024]{2,1,0:T(8,128)S(1)} collective-permute-done((f32[2,64,1024]{2,1,0:T(8,128)S(1)}, f32[2,64,1024]{2,1,0:T(8,128)S(1)}, u32[]{:S(2)}, u32[]{:S(2)}) %collective-permute-start.29) | collective-permute-done | bytes 524320 | tf_op jit(solution)/shard_map/ppermute | solution.py:12
  73.1 2.0 %convolution_subtract_fusion = f32[32,1024]{1,0:T(8,128)S(1)} fusion(f32[32,512]{1,0:T(8,128)S(1)} %add.304, f32[1024,512]{1,0:T(8,128)S(1)} %bitcast.191, f32[32,1024]{1,0:T(8,128)S(1)} %bitcast.209, pred[1024]{0:T(1024)(128)(4,1)S(1)} %broadcast_in_dim.136), kind=kOutput, calls=%fused_computation | convolution fusion | flops 201392128 | bytes 2425856 | tf_op jit(solution)/shard_map/dot_general | solution.py:68
  75.3 5.8 %collective-permute-done.25 = f32[32,1024]{1,0:T(8,128)S(1)} collective-permute-done((f32[32,1024]{1,0:T(8,128)S(1)}, f32[32,1024]{1,0:T(8,128)S(1)}, u32[]{:S(2)}, u32[]{:S(2)}) %collective-permute-start.25) | collective-permute-done | bytes 131104 | tf_op jit(solution)/shard_map/ppermute | solution.py:12
  81.1 2.4 %collective-permute-start.26 = (f32[32,1024]{1,0:T(8,128)S(1)}, f32[32,1024]{1,0:T(8,128)S(1)}, u32[]{:S(2)}, u32[]{:S(2)}) collective-permute-start(f32[32,1024]{1,0:T(8,128)S(1)} %add.311), channel_id=1, source_target_pairs={{0,24},{8,16},{16,8},{24,0},{1,25},{9,17},{17,9},{25,1},{2,26},{10... | collective-permute-start | bytes 393224 | tf_op jit(solution)/shard_map/ppermute | solution.py:12
  83.6 4.5 %collective-permute-done.26 = f32[32,1024]{1,0:T(8,128)S(1)} collective-permute-done((f32[32,1024]{1,0:T(8,128)S(1)}, f32[32,1024]{1,0:T(8,128)S(1)}, u32[]{:S(2)}, u32[]{:S(2)}) %collective-permute-start.26) | collective-permute-done | bytes 131104 | tf_op jit(solution)/shard_map/ppermute | solution.py:12
  88.2 2.0 %fusion.9 = f32[32,512]{1,0:T(8,128)S(1)} fusion(f32[512,1024]{1,0:T(8,128)S(1)} %bitcast.189, f32[32,1024]{1,0:T(8,128)S(1)} %add.311, f32[32,1024]{1,0:T(8,128)S(1)} %collective-permute-done.26), kind=kOutput, calls=%fused_computation.50 | convolution fusion | flops 201359360 | bytes 2424832 | tf_op jit(solution)/shard_map/dot_general | solution.py:68
  90.2 1.5 %collective-permute-start.31 = (f32[32,512]{1,0:T(8,128)S(1)}, f32[32,512]{1,0:T(8,128)S(1)}, u32[]{:S(2)}, u32[]{:S(2)}) collective-permute-start(f32[32,512]{1,0:T(8,128)S(1)} %fusion.9), channel_id=1, source_target_pairs={{0,4},{1,5},{2,6},{3,7},{4,0},{5,1},{6,2},{7,3},{8,12},{9,13},{10,... | collective-permute-start | bytes 196616 | tf_op jit(solution)/shard_map/ppermute | solution.py:12
  91.6 2.9 %collective-permute-done.31 = f32[32,512]{1,0:T(8,128)S(1)} collective-permute-done((f32[32,512]{1,0:T(8,128)S(1)}, f32[32,512]{1,0:T(8,128)S(1)}, u32[]{:S(2)}, u32[]{:S(2)}) %collective-permute-start.31) | collective-permute-done | bytes 65568 | tf_op jit(solution)/shard_map/ppermute | solution.py:12
  94.5 1.3 fusion.18
  95.8 1.5 %collective-permute-start.32 = (f32[32,1024]{1,0:T(8,128)S(1)}, f32[32,1024]{1,0:T(8,128)S(1)}, u32[]{:S(2)}, u32[]{:S(2)}) collective-permute-start(f32[32,1024]{1,0:T(8,128)S(1)} %fusion.18), channel_id=1, source_target_pairs={{0,8},{8,0},{16,24},{24,16},{1,9},{9,1},{17,25},{25,17},{2,10},{10... | collective-permute-start | bytes 393224 | tf_op jit(solution)/shard_map/ppermute | solution.py:12
  97.3 3.5 %collective-permute-done.32 = f32[32,1024]{1,0:T(8,128)S(1)} collective-permute-done((f32[32,1024]{1,0:T(8,128)S(1)}, f32[32,1024]{1,0:T(8,128)S(1)}, u32[]{:S(2)}, u32[]{:S(2)}) %collective-permute-start.32) | collective-permute-done | bytes 131104 | tf_op jit(solution)/shard_map/ppermute | solution.py:12
  100.8 2.4 %collective-permute-start.33 = (f32[32,1024]{1,0:T(8,128)S(1)}, f32[32,1024]{1,0:T(8,128)S(1)}, u32[]{:S(2)}, u32[]{:S(2)}) collective-permute-start(f32[32,1024]{1,0:T(8,128)S(1)} %add.326), channel_id=1, source_target_pairs={{0,24},{8,16},{16,8},{24,0},{1,25},{9,17},{17,9},{25,1},{2,26},{10... | collective-permute-start | bytes 393224 | tf_op jit(solution)/shard_map/ppermute | solution.py:12
  103.3 4.5 %collective-permute-done.33 = f32[32,1024]{1,0:T(8,128)S(1)} collective-permute-done((f32[32,1024]{1,0:T(8,128)S(1)}, f32[32,1024]{1,0:T(8,128)S(1)}, u32[]{:S(2)}, u32[]{:S(2)}) %collective-permute-start.33) | collective-permute-done | bytes 131104 | tf_op jit(solution)/shard_map/ppermute | solution.py:12
  107.8 1.5 %fusion.33 = f32[32,512]{1,0:T(8,128)S(1)} fusion(f32[32,1024]{1,0:T(8,128)S(1)} %add.327, f32[1024,512]{1,0:T(8,128)S(1)} %bitcast.192), kind=kOutput, calls=%fused_computation.136 | convolution fusion | flops 201326592 | bytes 2293760 | tf_op jit(solution)/shard_map/dot_general | solution.py:68
  109.3 1.5 %collective-permute-start.34 = (f32[32,512]{1,0:T(8,128)S(1)}, f32[32,512]{1,0:T(8,128)S(1)}, u32[]{:S(2)}, u32[]{:S(2)}) collective-permute-start(f32[32,512]{1,0:T(8,128)S(1)} %fusion.33), channel_id=1, source_target_pairs={{0,4},{1,5},{2,6},{3,7},{4,0},{5,1},{6,2},{7,3},{8,12},{9,13},{10,... | collective-permute-start | bytes 196616 | tf_op jit(solution)/shard_map/ppermute | solution.py:12
  110.7 2.9 %collective-permute-done.34 = f32[32,512]{1,0:T(8,128)S(1)} collective-permute-done((f32[32,512]{1,0:T(8,128)S(1)}, f32[32,512]{1,0:T(8,128)S(1)}, u32[]{:S(2)}, u32[]{:S(2)}) %collective-permute-start.34) | collective-permute-done | bytes 65568 | tf_op jit(solution)/shard_map/ppermute | solution.py:12
  114.3 1.3 %collective-permute-start.35 = (f32[32,512]{1,0:T(8,128)S(1)}, f32[32,512]{1,0:T(8,128)S(1)}, u32[]{:S(2)}, u32[]{:S(2)}) collective-permute-start(f32[32,512]{1,0:T(8,128)S(1)} %fusion.15), channel_id=1, source_target_pairs={{0,8},{8,0},{16,24},{24,16},{1,9},{9,1},{17,25},{25,17},{2,10},{10... | collective-permute-start | bytes 196616 | tf_op jit(solution)/shard_map/ppermute | solution.py:12
  115.6 3.0 %collective-permute-done.35 = f32[32,512]{1,0:T(8,128)S(1)} collective-permute-done((f32[32,512]{1,0:T(8,128)S(1)}, f32[32,512]{1,0:T(8,128)S(1)}, u32[]{:S(2)}, u32[]{:S(2)}) %collective-permute-start.35) | collective-permute-done | bytes 65568 | tf_op jit(solution)/shard_map/ppermute | solution.py:12
  119.5 1.3 collective-permute-start.41
  121.5 1.4 %collective-permute-start.36 = (f32[32,512]{1,0:T(8,128)S(1)}, f32[32,512]{1,0:T(8,128)S(1)}, u32[]{:S(2)}, u32[]{:S(2)}) collective-permute-start(f32[32,512]{1,0:T(8,128)S(1)} %fusion.34), channel_id=1, source_target_pairs={{0,4},{1,5},{2,6},{3,7},{4,0},{5,1},{6,2},{7,3},{8,12},{9,13},{10,... | collective-permute-start | bytes 196616 | tf_op jit(solution)/shard_map/ppermute | solution.py:12
  123.7 2.1 %collective-permute-done.36 = f32[32,512]{1,0:T(8,128)S(1)} collective-permute-done((f32[32,512]{1,0:T(8,128)S(1)}, f32[32,512]{1,0:T(8,128)S(1)}, u32[]{:S(2)}, u32[]{:S(2)}) %collective-permute-start.36) | collective-permute-done | bytes 65568 | tf_op jit(solution)/shard_map/ppermute | solution.py:12
  126.2 1.3 collective-permute-start.38
  128.2 1.2 collective-permute-done.39
  130.1 0.8 copy.37
  (162 shorter events, 14.5 us)
Async XLA Ops:
  0.0 10.1 %copy-start.7 = (s32[1,1,32]{2,1,0:T(1,128)S(1)}, s32[1,1,32]{2,1,0:T(1,128)}, u32[]{:S(2)}) copy-start(s32[1,1,32]{2,1,0:T(1,128)} %param.15) | copy-start | bytes 388
  0.0 10.1 %copy-start.8 = (s32[1,1,16]{2,1,0:T(1,128)S(1)}, s32[1,1,16]{2,1,0:T(1,128)}, u32[]{:S(2)}) copy-start(s32[1,1,16]{2,1,0:T(1,128)} %param.14) | copy-start | bytes 196
  0.0 10.4 %copy-start.1 = (f32[1,64,1024]{2,1,0:T(8,128)S(1)}, f32[1,64,1024]{2,1,0:T(8,128)}, u32[]{:S(2)}) copy-start(f32[1,64,1024]{2,1,0:T(8,128)} %param.12) | copy-start | bytes 786436
  0.0 11.2 %copy-start.4 = (f32[1,64,1024]{2,1,0:T(8,128)S(1)}, f32[1,64,1024]{2,1,0:T(8,128)}, u32[]{:S(2)}) copy-start(f32[1,64,1024]{2,1,0:T(8,128)} %param.10) | copy-start | bytes 786436
  1.0 15.1 %collective-permute-start.3 = (f32[64,256]{1,0:T(8,128)S(1)}, f32[64,256]{1,0:T(8,128)S(1)}, u32[]{:S(2)}, u32[]{:S(2)}) collective-permute-start(f32[64,256]{1,0:T(8,128)S(1)} %get-tuple-element.23), channel_id=1, source_target_pairs={{0,4},{1,5},{2,6},{3,7},{4,0},{5,1},{6,2},{7,3},{8,12},{9,13},{10,... | collective-permute-start | bytes 196616 | tf_op jit(solution)/shard_map/ppermute | solution.py:12
  4.1 13.7 %collective-permute-start.6 = (f32[64,256]{1,0:T(8,128)S(1)}, f32[64,256]{1,0:T(8,128)S(1)}, u32[]{:S(2)}, u32[]{:S(2)}) collective-permute-start(f32[64,256]{1,0:T(8,128)S(1)} %get-tuple-element.23), channel_id=1, source_target_pairs={{0,6},{1,7},{2,4},{3,5},{4,2},{5,3},{6,0},{7,1},{8,14},{9,15},{10,... | collective-permute-start | bytes 196616 | tf_op jit(solution)/shard_map/ppermute | solution.py:12
  7.4 33.0 %collective-permute-start.27 = (f32[64,1024]{1,0:T(8,128)}, f32[64,1024]{1,0:T(8,128)S(1)}, u32[]{:S(2)}, u32[]{:S(2)}) collective-permute-start(f32[64,1024]{1,0:T(8,128)} %pad_maximum_fusion.1), channel_id=1, source_target_pairs={{0,4},{1,5},{2,6},{3,7},{4,0},{5,1},{6,2},{7,3},{8,12},{9,13},{10,... | collective-permute-start | bytes 786440 | tf_op jit(solution)/shard_map/ppermute | solution.py:12
  9.2 3.6 %collective-permute-start.2 = (f32[3,32,64]{2,1,0:T(8,128)S(1)}, f32[3,32,64]{2,1,0:T(8,128)S(1)}, u32[]{:S(2)}, u32[]{:S(2)}) collective-permute-start(f32[3,32,64]{2,1,0:T(8,128)S(1)} %bitcast.227), channel_id=1, source_target_pairs={{0,3},{1,2},{2,1},{3,0},{4,7},{5,6},{6,5},{7,4},{8,11},{9,10},{10,... | collective-permute-start | bytes 73736 | tf_op jit(solution)/shard_map/ppermute | solution.py:12
  9.3 4.5 %collective-permute-start.1 = (f32[3,32,64]{2,1,0:T(8,128)S(1)}, f32[3,32,64]{2,1,0:T(8,128)S(1)}, u32[]{:S(2)}, u32[]{:S(2)}) collective-permute-start(f32[3,32,64]{2,1,0:T(8,128)S(1)} %bitcast.226), channel_id=1, source_target_pairs={{0,2},{1,3},{2,0},{3,1},{4,6},{5,7},{6,4},{7,5},{8,10},{9,11},{10,... | collective-permute-start | bytes 73736 | tf_op jit(solution)/shard_map/ppermute | solution.py:12
  12.7 23.1 %collective-permute-start.14 = (f32[64,512]{1,0:T(8,128)S(1)}, f32[64,512]{1,0:T(8,128)S(1)}, u32[]{:S(2)}, u32[]{:S(2)}) collective-permute-start(f32[64,512]{1,0:T(8,128)S(1)} %pad_maximum_fusion.3), channel_id=1, source_target_pairs={{0,4},{1,5},{2,6},{3,7},{4,0},{5,1},{6,2},{7,3},{8,12},{9,13},{10,... | collective-permute-start | bytes 393224 | tf_op jit(solution)/shard_map/ppermute | solution.py:12
  13.8 1.2 collective-permute-start
  15.0 5.4 %collective-permute-start.5 = (f32[64,256]{1,0:T(8,128)S(1)}, f32[64,256]{1,0:T(8,128)S(1)}, u32[]{:S(2)}, u32[]{:S(2)}) collective-permute-start(f32[64,256]{1,0:T(8,128)S(1)} %bitcast.201), channel_id=1, source_target_pairs={{0,2},{1,3},{2,0},{3,1},{4,6},{5,7},{6,4},{7,5},{8,10},{9,11},{10,... | collective-permute-start | bytes 196616 | tf_op jit(solution)/shard_map/ppermute | solution.py:12
  16.1 20.5 %collective-permute-start.9 = (f32[64,512]{1,0:T(8,128)}, f32[64,512]{1,0:T(8,128)S(1)}, u32[]{:S(2)}, u32[]{:S(2)}) collective-permute-start(f32[64,512]{1,0:T(8,128)} %bitcast_multiply_fusion.3), channel_id=1, source_target_pairs={{0,8},{8,0},{16,24},{24,16},{1,9},{9,1},{17,25},{25,17},{2,10},{10... | collective-permute-start | bytes 393224 | tf_op jit(solution)/shard_map/ppermute | solution.py:12
  17.8 18.0 %copy-start.5 = (f32[64,256]{1,0:T(8,128)}, f32[64,256]{1,0:T(8,128)S(1)}, u32[]{:S(2)}) copy-start(f32[64,256]{1,0:T(8,128)S(1)} %collective-permute-done.6) | copy-start | bytes 196612
  17.8 13.0 %collective-permute-start.20 = (f32[64,512]{1,0:T(8,128)S(1)}, f32[64,512]{1,0:T(8,128)S(1)}, u32[]{:S(2)}, u32[]{:S(2)}) collective-permute-start(f32[64,512]{1,0:T(8,128)S(1)} %get-tuple-element.7), channel_id=1, source_target_pairs={{0,16},{8,24},{16,0},{24,8},{1,17},{9,25},{17,1},{25,9},{2,18},{10... | collective-permute-start | bytes 393224 | tf_op jit(solution)/shard_map/ppermute | solution.py:12
  20.4 10.3 %collective-permute-start.21 = (f32[64,512]{1,0:T(8,128)S(1)}, f32[64,512]{1,0:T(8,128)S(1)}, u32[]{:S(2)}, u32[]{:S(2)}) collective-permute-start(f32[64,512]{1,0:T(8,128)S(1)} %get-tuple-element.6), channel_id=1, source_target_pairs={{0,24},{8,16},{16,8},{24,0},{1,25},{9,17},{17,9},{25,1},{2,26},{10... | collective-permute-start | bytes 393224 | tf_op jit(solution)/shard_map/ppermute | solution.py:12
  30.8 5.0 %collective-permute-start.19 = (f32[64,512]{1,0:T(8,128)S(1)}, f32[64,512]{1,0:T(8,128)S(1)}, u32[]{:S(2)}, u32[]{:S(2)}) collective-permute-start(f32[64,512]{1,0:T(8,128)S(1)} %get-tuple-element.5), channel_id=1, source_target_pairs={{0,8},{8,0},{16,24},{24,16},{1,9},{9,1},{17,25},{25,17},{2,10},{10... | collective-permute-start | bytes 393224 | tf_op jit(solution)/shard_map/ppermute | solution.py:12
  30.8 7.6 %collective-permute-start.4 = (f32[2,64,256]{2,1,0:T(8,128)S(1)}, f32[2,64,256]{2,1,0:T(8,128)S(1)}, u32[]{:S(2)}, u32[]{:S(2)}) collective-permute-start(f32[2,64,256]{2,1,0:T(8,128)S(1)} %maximum_select_fusion.11), channel_id=1, source_target_pairs={{0,1},{1,0},{2,3},{3,2},{4,5},{5,4},{6,7},{7,6},{8,9},{9,8},{10,11... | collective-permute-start | bytes 393224 | tf_op jit(solution)/shard_map/ppermute | solution.py:12
  35.8 3.2 %collective-permute-start.7 = (f32[2,64,256]{2,1,0:T(8,128)S(1)}, f32[2,64,256]{2,1,0:T(8,128)S(1)}, u32[]{:S(2)}, u32[]{:S(2)}) collective-permute-start(f32[2,64,256]{2,1,0:T(8,128)S(1)} %maximum_select_fusion.13), channel_id=1, source_target_pairs={{0,1},{1,0},{2,3},{3,2},{4,5},{5,4},{6,7},{7,6},{8,9},{9,8},{10,11... | collective-permute-start | bytes 393224 | tf_op jit(solution)/shard_map/ppermute | solution.py:12
  35.9 15.6 %collective-permute-start.15 = (f32[2,64,512]{2,1,0:T(8,128)S(1)}, f32[2,64,512]{2,1,0:T(8,128)S(1)}, u32[]{:S(2)}, u32[]{:S(2)}) collective-permute-start(f32[2,64,512]{2,1,0:T(8,128)S(1)} %maximum_select_fusion.7), channel_id=1, source_target_pairs={{0,1},{1,0},{2,3},{3,2},{4,5},{5,4},{6,7},{7,6},{8,9},{9,8},{10,11... | collective-permute-start | bytes 786440 | tf_op jit(solution)/shard_map/ppermute | solution.py:12
  36.6 15.5 %collective-permute-start.16 = (f32[2,64,512]{2,1,0:T(8,128)S(1)}, f32[2,64,512]{2,1,0:T(8,128)S(1)}, u32[]{:S(2)}, u32[]{:S(2)}) collective-permute-start(f32[2,64,512]{2,1,0:T(8,128)S(1)} %maximum_select_fusion.7), channel_id=1, source_target_pairs={{0,2},{1,3},{2,0},{3,1},{4,6},{5,7},{6,4},{7,5},{8,10},{9,11},{10,... | collective-permute-start | bytes 786440 | tf_op jit(solution)/shard_map/ppermute | solution.py:12
  38.4 6.4 %collective-permute-start.10 = (f32[2,64,512]{2,1,0:T(8,128)S(1)}, f32[2,64,512]{2,1,0:T(8,128)S(1)}, u32[]{:S(2)}, u32[]{:S(2)}) collective-permute-start(f32[2,64,512]{2,1,0:T(8,128)S(1)} %maximum_select_fusion.5), channel_id=1, source_target_pairs={{0,1},{1,0},{2,3},{3,2},{4,5},{5,4},{6,7},{7,6},{8,9},{9,8},{10,11... | collective-permute-start | bytes 786440 | tf_op jit(solution)/shard_map/ppermute | solution.py:12
  38.9 12.5 %collective-permute-start.11 = (f32[2,64,512]{2,1,0:T(8,128)S(1)}, f32[2,64,512]{2,1,0:T(8,128)S(1)}, u32[]{:S(2)}, u32[]{:S(2)}) collective-permute-start(f32[2,64,512]{2,1,0:T(8,128)S(1)} %maximum_select_fusion.5), channel_id=1, source_target_pairs={{0,2},{1,3},{2,0},{3,1},{4,6},{5,7},{6,4},{7,5},{8,10},{9,11},{10,... | collective-permute-start | bytes 786440 | tf_op jit(solution)/shard_map/ppermute | solution.py:12
  40.4 4.3 %collective-permute-start.8 = (f32[32,512]{1,0:T(8,128)S(1)}, f32[32,512]{1,0:T(8,128)S(1)}, u32[]{:S(2)}, u32[]{:S(2)}) collective-permute-start(f32[32,512]{1,0:T(8,128)S(1)} %fusion.23), channel_id=1, source_target_pairs={{0,4},{1,5},{2,6},{3,7},{4,0},{5,1},{6,2},{7,3},{8,12},{9,13},{10,... | collective-permute-start | bytes 196616 | tf_op jit(solution)/shard_map/ppermute | solution.py:12
  44.8 10.2 %collective-permute-start.22 = (f32[4,64,512]{2,1,0:T(8,128)S(1)}, f32[4,64,512]{2,1,0:T(8,128)S(1)}, u32[]{:S(2)}, u32[]{:S(2)}) collective-permute-start(f32[4,64,512]{2,1,0:T(8,128)S(1)} %maximum_select_fusion.1), channel_id=1, source_target_pairs={{0,1},{1,0},{2,3},{3,2},{4,5},{5,4},{6,7},{7,6},{8,9},{9,8},{10,11... | collective-permute-start | bytes 1572872 | tf_op jit(solution)/shard_map/ppermute | solution.py:12
  44.8 17.9 %collective-permute-start.23 = (f32[4,64,512]{2,1,0:T(8,128)S(1)}, f32[4,64,512]{2,1,0:T(8,128)S(1)}, u32[]{:S(2)}, u32[]{:S(2)}) collective-permute-start(f32[4,64,512]{2,1,0:T(8,128)S(1)} %maximum_select_fusion.1), channel_id=1, source_target_pairs={{0,2},{1,3},{2,0},{3,1},{4,6},{5,7},{6,4},{7,5},{8,10},{9,11},{10,... | collective-permute-start | bytes 1572872 | tf_op jit(solution)/shard_map/ppermute | solution.py:12
  51.5 21.6 %collective-permute-start.28 = (f32[2,64,1024]{2,1,0:T(8,128)S(1)}, f32[2,64,1024]{2,1,0:T(8,128)S(1)}, u32[]{:S(2)}, u32[]{:S(2)}) collective-permute-start(f32[2,64,1024]{2,1,0:T(8,128)S(1)} %maximum_select_fusion.3), channel_id=1, source_target_pairs={{0,1},{1,0},{2,3},{3,2},{4,5},{5,4},{6,7},{7,6},{8,9},{9,8},{10,11... | collective-permute-start | bytes 1572872 | tf_op jit(solution)/shard_map/ppermute | solution.py:12
  51.5 2.2 %collective-permute-start.12 = (f32[2,64,512]{2,1,0:T(8,128)S(1)}, f32[2,64,512]{2,1,0:T(8,128)S(1)}, u32[]{:S(2)}, u32[]{:S(2)}) collective-permute-start(f32[2,64,512]{2,1,0:T(8,128)S(1)} %collective-permute-done.11), channel_id=1, source_target_pairs={{0,1},{1,0},{2,3},{3,2},{4,5},{5,4},{6,7},{7,6},{8,9},{9,8},{10,11... | collective-permute-start | bytes 786440 | tf_op jit(solution)/shard_map/ppermute | solution.py:12
  52.1 20.9 %collective-permute-start.29 = (f32[2,64,1024]{2,1,0:T(8,128)S(1)}, f32[2,64,1024]{2,1,0:T(8,128)S(1)}, u32[]{:S(2)}, u32[]{:S(2)}) collective-permute-start(f32[2,64,1024]{2,1,0:T(8,128)S(1)} %maximum_select_fusion.3), channel_id=1, source_target_pairs={{0,2},{1,3},{2,0},{3,1},{4,6},{5,7},{6,4},{7,5},{8,10},{9,11},{10,... | collective-permute-start | bytes 1572872 | tf_op jit(solution)/shard_map/ppermute | solution.py:12
  53.7 9.0 %collective-permute-start.17 = (f32[2,64,512]{2,1,0:T(8,128)S(1)}, f32[2,64,512]{2,1,0:T(8,128)S(1)}, u32[]{:S(2)}, u32[]{:S(2)}) collective-permute-start(f32[2,64,512]{2,1,0:T(8,128)S(1)} %collective-permute-done.16), channel_id=1, source_target_pairs={{0,1},{1,0},{2,3},{3,2},{4,5},{5,4},{6,7},{7,6},{8,9},{9,8},{10,11... | collective-permute-start | bytes 786440 | tf_op jit(solution)/shard_map/ppermute | solution.py:12
  55.0 7.8 %collective-permute-start.13 = (f32[32,512]{1,0:T(8,128)S(1)}, f32[32,512]{1,0:T(8,128)S(1)}, u32[]{:S(2)}, u32[]{:S(2)}) collective-permute-start(f32[32,512]{1,0:T(8,128)S(1)} %convolution_subtract_fusion.1), channel_id=1, source_target_pairs={{0,8},{8,0},{16,24},{24,16},{1,9},{9,1},{17,25},{25,17},{2,10},{10... | collective-permute-start | bytes 196616 | tf_op jit(solution)/shard_map/ppermute | solution.py:12
  62.7 10.4 %collective-permute-start.24 = (f32[4,64,512]{2,1,0:T(8,128)S(1)}, f32[4,64,512]{2,1,0:T(8,128)S(1)}, u32[]{:S(2)}, u32[]{:S(2)}) collective-permute-start(f32[4,64,512]{2,1,0:T(8,128)S(1)} %collective-permute-done.23), channel_id=1, source_target_pairs={{0,1},{1,0},{2,3},{3,2},{4,5},{5,4},{6,7},{7,6},{8,9},{9,8},{10,11... | collective-permute-start | bytes 1572872 | tf_op jit(solution)/shard_map/ppermute | solution.py:12
  63.8 9.1 %collective-permute-start.18 = (f32[32,512]{1,0:T(8,128)S(1)}, f32[32,512]{1,0:T(8,128)S(1)}, u32[]{:S(2)}, u32[]{:S(2)}) collective-permute-start(f32[32,512]{1,0:T(8,128)S(1)} %fusion.20), channel_id=1, source_target_pairs={{0,4},{1,5},{2,6},{3,7},{4,0},{5,1},{6,2},{7,3},{8,12},{9,13},{10,... | collective-permute-start | bytes 196616 | tf_op jit(solution)/shard_map/ppermute | solution.py:12
  73.0 10.6 %collective-permute-start.30 = (f32[2,64,1024]{2,1,0:T(8,128)S(1)}, f32[2,64,1024]{2,1,0:T(8,128)S(1)}, u32[]{:S(2)}, u32[]{:S(2)}) collective-permute-start(f32[2,64,1024]{2,1,0:T(8,128)S(1)} %collective-permute-done.29), channel_id=1, source_target_pairs={{0,1},{1,0},{2,3},{3,2},{4,5},{5,4},{6,7},{7,6},{8,9},{9,8},{10,11... | collective-permute-start | bytes 1572872 | tf_op jit(solution)/shard_map/ppermute | solution.py:12
  75.1 6.0 %collective-permute-start.25 = (f32[32,1024]{1,0:T(8,128)S(1)}, f32[32,1024]{1,0:T(8,128)S(1)}, u32[]{:S(2)}, u32[]{:S(2)}) collective-permute-start(f32[32,1024]{1,0:T(8,128)S(1)} %convolution_subtract_fusion), channel_id=1, source_target_pairs={{0,8},{8,0},{16,24},{24,16},{1,9},{9,1},{17,25},{25,17},{2,10},{10... | collective-permute-start | bytes 393224 | tf_op jit(solution)/shard_map/ppermute | solution.py:12
  81.1 7.0 %collective-permute-start.26 = (f32[32,1024]{1,0:T(8,128)S(1)}, f32[32,1024]{1,0:T(8,128)S(1)}, u32[]{:S(2)}, u32[]{:S(2)}) collective-permute-start(f32[32,1024]{1,0:T(8,128)S(1)} %add.311), channel_id=1, source_target_pairs={{0,24},{8,16},{16,8},{24,0},{1,25},{9,17},{17,9},{25,1},{2,26},{10... | collective-permute-start | bytes 393224 | tf_op jit(solution)/shard_map/ppermute | solution.py:12
  90.2 4.3 %collective-permute-start.31 = (f32[32,512]{1,0:T(8,128)S(1)}, f32[32,512]{1,0:T(8,128)S(1)}, u32[]{:S(2)}, u32[]{:S(2)}) collective-permute-start(f32[32,512]{1,0:T(8,128)S(1)} %fusion.9), channel_id=1, source_target_pairs={{0,4},{1,5},{2,6},{3,7},{4,0},{5,1},{6,2},{7,3},{8,12},{9,13},{10,... | collective-permute-start | bytes 196616 | tf_op jit(solution)/shard_map/ppermute | solution.py:12
  95.8 5.0 %collective-permute-start.32 = (f32[32,1024]{1,0:T(8,128)S(1)}, f32[32,1024]{1,0:T(8,128)S(1)}, u32[]{:S(2)}, u32[]{:S(2)}) collective-permute-start(f32[32,1024]{1,0:T(8,128)S(1)} %fusion.18), channel_id=1, source_target_pairs={{0,8},{8,0},{16,24},{24,16},{1,9},{9,1},{17,25},{25,17},{2,10},{10... | collective-permute-start | bytes 393224 | tf_op jit(solution)/shard_map/ppermute | solution.py:12
  100.8 6.9 %collective-permute-start.33 = (f32[32,1024]{1,0:T(8,128)S(1)}, f32[32,1024]{1,0:T(8,128)S(1)}, u32[]{:S(2)}, u32[]{:S(2)}) collective-permute-start(f32[32,1024]{1,0:T(8,128)S(1)} %add.326), channel_id=1, source_target_pairs={{0,24},{8,16},{16,8},{24,0},{1,25},{9,17},{17,9},{25,1},{2,26},{10... | collective-permute-start | bytes 393224 | tf_op jit(solution)/shard_map/ppermute | solution.py:12
  109.3 4.3 %collective-permute-start.34 = (f32[32,512]{1,0:T(8,128)S(1)}, f32[32,512]{1,0:T(8,128)S(1)}, u32[]{:S(2)}, u32[]{:S(2)}) collective-permute-start(f32[32,512]{1,0:T(8,128)S(1)} %fusion.33), channel_id=1, source_target_pairs={{0,4},{1,5},{2,6},{3,7},{4,0},{5,1},{6,2},{7,3},{8,12},{9,13},{10,... | collective-permute-start | bytes 196616 | tf_op jit(solution)/shard_map/ppermute | solution.py:12
  114.3 4.3 %collective-permute-start.35 = (f32[32,512]{1,0:T(8,128)S(1)}, f32[32,512]{1,0:T(8,128)S(1)}, u32[]{:S(2)}, u32[]{:S(2)}) collective-permute-start(f32[32,512]{1,0:T(8,128)S(1)} %fusion.15), channel_id=1, source_target_pairs={{0,8},{8,0},{16,24},{24,16},{1,9},{9,1},{17,25},{25,17},{2,10},{10... | collective-permute-start | bytes 196616 | tf_op jit(solution)/shard_map/ppermute | solution.py:12
  119.5 3.5 %collective-permute-start.42 = (f32[2,32,64]{2,1,0:T(8,128)S(1)}, f32[2,32,64]{2,1,0:T(8,128)S(1)}, u32[]{:S(2)}, u32[]{:S(2)}) collective-permute-start(f32[2,32,64]{2,1,0:T(8,128)S(1)} %get-tuple-element.39), channel_id=1, source_target_pairs={{0,3},{1,2},{2,1},{3,0},{4,7},{5,6},{6,5},{7,4},{8,11},{9,10},{10,... | collective-permute-start | bytes 49160 | tf_op jit(solution)/shard_map/ppermute | solution.py:12
  119.5 4.1 %collective-permute-start.41 = (f32[2,32,64]{2,1,0:T(8,128)S(1)}, f32[2,32,64]{2,1,0:T(8,128)S(1)}, u32[]{:S(2)}, u32[]{:S(2)}) collective-permute-start(f32[2,32,64]{2,1,0:T(8,128)S(1)} %get-tuple-element.38), channel_id=1, source_target_pairs={{0,2},{1,3},{2,0},{3,1},{4,6},{5,7},{6,4},{7,5},{8,10},{9,11},{10,... | collective-permute-start | bytes 49160 | tf_op jit(solution)/shard_map/ppermute | solution.py:12
  120.9 2.7 %collective-permute-start.40 = (f32[2,32,64]{2,1,0:T(8,128)S(1)}, f32[2,32,64]{2,1,0:T(8,128)S(1)}, u32[]{:S(2)}, u32[]{:S(2)}) collective-permute-start(f32[2,32,64]{2,1,0:T(8,128)S(1)} %get-tuple-element.37), channel_id=1, source_target_pairs={{0,1},{1,0},{2,3},{3,2},{4,5},{5,4},{6,7},{7,6},{8,9},{9,8},{10,11... | collective-permute-start | bytes 49160 | tf_op jit(solution)/shard_map/ppermute | solution.py:12
  121.5 4.3 %collective-permute-start.36 = (f32[32,512]{1,0:T(8,128)S(1)}, f32[32,512]{1,0:T(8,128)S(1)}, u32[]{:S(2)}, u32[]{:S(2)}) collective-permute-start(f32[32,512]{1,0:T(8,128)S(1)} %fusion.34), channel_id=1, source_target_pairs={{0,4},{1,5},{2,6},{3,7},{4,0},{5,1},{6,2},{7,3},{8,12},{9,13},{10,... | collective-permute-start | bytes 196616 | tf_op jit(solution)/shard_map/ppermute | solution.py:12
  126.2 3.2 %collective-permute-start.39 = (f32[1,32,64]{2,1,0:T(8,128)S(1)}, f32[1,32,64]{2,1,0:T(8,128)S(1)}, u32[]{:S(2)}, u32[]{:S(2)}) collective-permute-start(f32[1,32,64]{2,1,0:T(8,128)S(1)} %get-tuple-element.43), channel_id=1, source_target_pairs={{0,3},{1,2},{2,1},{3,0},{4,7},{5,6},{6,5},{7,4},{8,11},{9,10},{10,... | collective-permute-start | bytes 24584 | tf_op jit(solution)/shard_map/ppermute | solution.py:12
  126.2 3.8 %collective-permute-start.38 = (f32[1,32,64]{2,1,0:T(8,128)S(1)}, f32[1,32,64]{2,1,0:T(8,128)S(1)}, u32[]{:S(2)}, u32[]{:S(2)}) collective-permute-start(f32[1,32,64]{2,1,0:T(8,128)S(1)} %get-tuple-element.42), channel_id=1, source_target_pairs={{0,2},{1,3},{2,0},{3,1},{4,6},{5,7},{6,4},{7,5},{8,10},{9,11},{10,... | collective-permute-start | bytes 24584 | tf_op jit(solution)/shard_map/ppermute | solution.py:12
  127.6 2.5 %collective-permute-start.37 = (f32[1,32,64]{2,1,0:T(8,128)S(1)}, f32[1,32,64]{2,1,0:T(8,128)S(1)}, u32[]{:S(2)}, u32[]{:S(2)}) collective-permute-start(f32[1,32,64]{2,1,0:T(8,128)S(1)} %get-tuple-element.41), channel_id=1, source_target_pairs={{0,1},{1,0},{2,3},{3,2},{4,5},{5,4},{6,7},{7,6},{8,9},{9,8},{10,11... | collective-permute-start | bytes 24584 | tf_op jit(solution)/shard_map/ppermute | solution.py:12
  (4 other events, 16.7 us)
